TPU v7x, 32 devices: a whole 2x2x4 slice. The times are simulated.
32 devices in a mesh: dp: 16 (over z, y, x), mp: 2 (over core).
Axes of the slice: x: 2, y: 2, z: 4, core: 2. Of those that a mesh axis runs over, the one named last changes fastest.
Arguments:
- inputs: bfloat16 [32, 512, 768], P('dp'), may hold values from -6 to 6
- counts: int32 [32], P('dp'), may hold values from 16 to 128, as said below
- w_qkv: bfloat16 [768, 3, 768], P(None, None, 'mp'), may hold values from -0.21875 to 0.21875
- w_out: bfloat16 [768, 768], P('mp'), may hold values from -2 to 2
- w_up: bfloat16 [768, 3072], P(None, 'mp'), may hold values from -0.21875 to 0.21875
- w_down: bfloat16 [3072, 768], P('mp'), may hold values from -0.109375 to 0.109375
- gain_one: float32 [768], replicated, may hold values from 0.1 to 1.9
- shift_one: float32 [768], replicated, may hold values from -3 to 3
- gain_two: float32 [768], replicated, may hold values from 0.1 to 1.9
- shift_two: float32 [768], replicated, may hold values from -3 to 3
- cotangent: bfloat16 [32, 512, 768], P('dp'), may hold values from -6 to 6
Outputs:
- outputs: bfloat16 [32, 512, 768], P('dp')
- grad_inputs: float32 [32, 512, 768], P('dp')
- grad_w_qkv: float32 [768, 3, 768], P('dp', None, 'mp')
- grad_w_out: float32 [768, 768], P('mp', 'dp')
- grad_w_up: float32 [768, 3072], P('dp', 'mp')
- grad_w_down: float32 [3072, 768], P('mp', 'dp')
- grad_gain_one: float32 [768], P('dp')
- grad_shift_one: float32 [768], P('dp')
- grad_gain_two: float32 [768], P('dp')
- grad_shift_two: float32 [768], P('dp')
Inputs may be any that keep to these rules, and one draw needn't show every extreme that they name: counts[t] is the number of live query rows of table t; some table has exactly 128.
All inputs are finite; a program needn't handle non-finite values.
Results may differ from a plain program's by a relative error of at most 0.015.
The roundings to bfloat16 on the way count: a program that leaves them out, or rounds other values in their place, can miss the bound.
Values may be sent and summed in bfloat16 or wider, within the bound.
A program may use at most 128 MiB of HBM per device.

v0:
```python
from functools import partial
import math

import jax
import jax.numpy as jnp
from jax import lax
from jax.sharding import PartitionSpec as P

HD = 64
CTX = 384


EPSILON = 1e-05


def layer_norm(row_data, norm_gain, norm_shift):
    centre = jnp.mean(row_data, axis=-1, keepdims=True)
    centred = row_data - centre
    inverse = lax.rsqrt(jnp.mean(centred * centred, axis=-1, keepdims=True) + EPSILON)
    unit_rows = centred * inverse
    return (unit_rows, inverse, unit_rows * norm_gain + norm_shift)


def norm_backward(grad_norm, unit_rows, inverse, norm_gain):
    grad_unit = grad_norm * norm_gain
    grad_mean = jnp.mean(grad_unit, axis=-1, keepdims=True)
    cross_mean = jnp.mean(grad_unit * unit_rows, axis=-1, keepdims=True)
    return inverse * (grad_unit - grad_mean - unit_rows * cross_mean)


def attend_forward(query_all, key_rows, value_rows, block_rows, score_scale):
    seq_len, heads_dev, head_dim = query_all.shape
    blocks = query_all.reshape(seq_len // block_rows, block_rows, heads_dev, head_dim)

    def one_block(query_block):
        scores = (
            jnp.einsum("bhd,khd->hbk", query_block, key_rows, preferred_element_type=jnp.float32)
            * score_scale
        )
        row_peak = jnp.max(scores, axis=-1, keepdims=True)
        exp_scores = jnp.exp(scores - row_peak)
        row_total = jnp.sum(exp_scores, axis=-1, keepdims=True)
        weights = (exp_scores / row_total).astype(jnp.bfloat16)
        block_out = jnp.einsum(
            "hbk,khd->bhd", weights, value_rows, preferred_element_type=jnp.float32
        )
        return (block_out.astype(jnp.bfloat16), row_peak + jnp.log(row_total))

    heads_out, log_total = lax.map(one_block, blocks)
    return (heads_out.reshape(seq_len, heads_dev * head_dim), log_total)


def attend_backward(
    query_all, key_rows, value_rows, grad_heads, log_total, block_rows, score_scale
):
    seq_len, heads_dev, head_dim = query_all.shape
    count_blocks = seq_len // block_rows
    query_blocks = query_all.reshape(count_blocks, block_rows, heads_dev, head_dim)
    grad_blocks = grad_heads.reshape(count_blocks, block_rows, heads_dev, head_dim)

    def one_block(running, block_items):
        query_block, grad_block, lse_block = block_items
        scores = (
            jnp.einsum("bhd,khd->hbk", query_block, key_rows, preferred_element_type=jnp.float32)
            * score_scale
        )
        softmax_rows = jnp.exp(scores - lse_block)
        grad_weights = jnp.einsum(
            "bhd,khd->hbk", grad_block, value_rows, preferred_element_type=jnp.float32
        )
        row_inner = jnp.sum(softmax_rows * grad_weights, axis=-1, keepdims=True)
        grad_scores = (softmax_rows * (grad_weights - row_inner)).astype(jnp.bfloat16)
        grad_query = (
            jnp.einsum("hbk,khd->bhd", grad_scores, key_rows, preferred_element_type=jnp.float32)
            * score_scale
        ).astype(jnp.bfloat16)
        grad_key = (
            running[0]
            + jnp.einsum(
                "hbk,bhd->khd", grad_scores, query_block, preferred_element_type=jnp.float32
            )
            * score_scale
        )
        grad_value = running[1] + jnp.einsum(
            "hbk,bhd->khd",
            softmax_rows.astype(jnp.bfloat16),
            grad_block,
            preferred_element_type=jnp.float32,
        )
        return ((grad_key, grad_value), grad_query)

    empty_grad = jnp.zeros(key_rows.shape, jnp.float32)
    (grad_key, grad_value), grad_query = lax.scan(
        one_block, (empty_grad, empty_grad), (query_blocks, grad_blocks, log_total)
    )
    return (
        grad_query.reshape(seq_len, heads_dev * head_dim),
        grad_key.astype(jnp.bfloat16),
        grad_value.astype(jnp.bfloat16),
    )


def reduce_total(grads):
    return (
        lax.psum_scatter(grads[0], "dp", scatter_dimension=0, tiled=True),
        lax.psum_scatter(grads[1], "dp", scatter_dimension=1, tiled=True),
        lax.psum_scatter(grads[2], "dp", scatter_dimension=0, tiled=True),
        lax.psum_scatter(grads[3], "dp", scatter_dimension=1, tiled=True),
        lax.psum_scatter(grads[4], "dp", scatter_dimension=0, tiled=True),
        lax.psum_scatter(grads[5], "dp", scatter_dimension=0, tiled=True),
        lax.psum_scatter(grads[6], "dp", scatter_dimension=0, tiled=True),
        lax.psum_scatter(grads[7], "dp", scatter_dimension=0, tiled=True),
    )


def per_device(
    inputs, counts, w_qkv, w_out, w_up, w_down, gain_one, shift_one, gain_two, shift_two, cotangent
):
    table_count, seq_len, width = inputs.shape
    heads_dev = w_out.shape[0] // HD
    block_rows = min(512, seq_len)
    score_scale = 1.0 / math.sqrt(HD)
    positions = jnp.arange(seq_len, dtype=jnp.int32)
    results = []
    grad_list = []
    totals = None
    for table_index in range(table_count):
        row_data = inputs[table_index].astype(jnp.float32)
        live_rows = (positions < CTX + counts[table_index]).astype(jnp.float32)[:, None]
        unit_one, inverse_one, normed = layer_norm(row_data, gain_one, shift_one)
        normed = normed.astype(jnp.bfloat16)
        context = normed[:CTX]
        query_all = (
            jnp.dot(normed, w_qkv[:, 0], preferred_element_type=jnp.float32)
            .astype(jnp.bfloat16)
            .reshape(seq_len, heads_dev, HD)
        )
        key_value = jnp.einsum(
            "sd,dcn->csn", context, w_qkv[:, 1:], preferred_element_type=jnp.float32
        ).astype(jnp.bfloat16)
        key_rows = key_value[0].reshape(CTX, heads_dev, HD)
        value_rows = key_value[1].reshape(CTX, heads_dev, HD)
        heads_out, log_total = attend_forward(
            query_all, key_rows, value_rows, block_rows, score_scale
        )
        attended = lax.psum(
            jnp.dot(heads_out, w_out, preferred_element_type=jnp.float32).astype(jnp.bfloat16), "mp"
        ).astype(jnp.float32)
        resid = row_data + attended
        unit_two, inverse_two, normed_two = layer_norm(resid, gain_two, shift_two)
        normed_two = normed_two.astype(jnp.bfloat16)
        lifted = jnp.dot(normed_two, w_up, preferred_element_type=jnp.float32)
        active_full, gelu_back = jax.vjp(partial(jax.nn.gelu, approximate=False), lifted)
        active = active_full.astype(jnp.bfloat16)
        mlp_out = lax.psum(
            jnp.dot(active, w_down, preferred_element_type=jnp.float32).astype(jnp.bfloat16), "mp"
        ).astype(jnp.float32)
        results.append(((resid + mlp_out) * live_rows).astype(jnp.bfloat16))
        grad_out = cotangent[table_index].astype(jnp.float32) * live_rows
        grad_low = grad_out.astype(jnp.bfloat16)
        grad_down = jnp.einsum("sf,sd->fd", active, grad_low, preferred_element_type=jnp.float32)
        grad_active = jnp.einsum("sd,fd->sf", grad_low, w_down, preferred_element_type=jnp.float32)
        grad_lifted = gelu_back(grad_active)[0].astype(jnp.bfloat16)
        grad_up = jnp.einsum(
            "sd,sf->df", normed_two, grad_lifted, preferred_element_type=jnp.float32
        )
        grad_norm_two = lax.psum(
            jnp.einsum("sf,df->sd", grad_lifted, w_up, preferred_element_type=jnp.float32).astype(
                jnp.bfloat16
            ),
            "mp",
        ).astype(jnp.float32)
        grad_gain_two = jnp.sum(grad_norm_two * unit_two, axis=0)
        grad_shift_two = jnp.sum(grad_norm_two, axis=0)
        grad_resid = grad_out + norm_backward(grad_norm_two, unit_two, inverse_two, gain_two)
        grad_attn = grad_resid.astype(jnp.bfloat16)
        grad_wout = jnp.einsum(
            "sk,sd->kd", heads_out, grad_attn, preferred_element_type=jnp.float32
        )
        grad_heads = (
            jnp.einsum("sd,kd->sk", grad_attn, w_out, preferred_element_type=jnp.float32)
            .astype(jnp.bfloat16)
            .reshape(seq_len, heads_dev, HD)
        )
        grad_query, grad_key, grad_value = attend_backward(
            query_all, key_rows, value_rows, grad_heads, log_total, block_rows, score_scale
        )
        grad_pairs = jnp.stack(
            [grad_key.reshape(CTX, heads_dev * HD), grad_value.reshape(CTX, heads_dev * HD)]
        )
        grad_wqkv = jnp.concatenate(
            [
                jnp.einsum("sd,sn->dn", normed, grad_query, preferred_element_type=jnp.float32)[
                    :, None
                ],
                jnp.einsum("sd,csn->dcn", context, grad_pairs, preferred_element_type=jnp.float32),
            ],
            axis=1,
        )
        context_part = jnp.einsum(
            "csn,dcn->sd", grad_pairs, w_qkv[:, 1:], preferred_element_type=jnp.float32
        )
        grad_norm_part = jnp.einsum(
            "sn,dn->sd", grad_query, w_qkv[:, 0], preferred_element_type=jnp.float32
        )
        grad_norm_part = grad_norm_part + jnp.concatenate(
            [context_part, jnp.zeros((seq_len - CTX, width), jnp.float32)], axis=0
        )
        grad_norm_one = lax.psum(grad_norm_part.astype(jnp.bfloat16), "mp").astype(jnp.float32)
        grad_gain_one = jnp.sum(grad_norm_one * unit_one, axis=0)
        grad_shift_one = jnp.sum(grad_norm_one, axis=0)
        grad_list.append(grad_resid + norm_backward(grad_norm_one, unit_one, inverse_one, gain_one))
        table_grads = (
            grad_wqkv,
            grad_wout,
            grad_up,
            grad_down,
            grad_gain_one,
            grad_shift_one,
            grad_gain_two,
            grad_shift_two,
        )
        totals = table_grads if totals is None else jax.tree.map(jnp.add, totals, table_grads)
    totals = reduce_total(totals)
    return (
        jnp.stack(results),
        jnp.stack(grad_list),
        totals[0],
        totals[1],
        totals[2],
        totals[3],
        totals[4],
        totals[5],
        totals[6],
        totals[7],
    )


def solution(mesh):
    in_specs = (
        P("dp", None, None),
        P("dp"),
        P(None, None, "mp"),
        P("mp", None),
        P(None, "mp"),
        P("mp", None),
        P(),
        P(),
        P(),
        P(),
        P("dp", None, None),
    )
    out_specs = (
        P("dp", None, None),
        P("dp", None, None),
        P("dp", None, "mp"),
        P("mp", "dp"),
        P("dp", "mp"),
        P("mp", "dp"),
        P("dp"),
        P("dp"),
        P("dp"),
        P("dp"),
    )
    return jax.shard_map(
        per_device, mesh=mesh, in_specs=in_specs, out_specs=out_specs, check_vma=False
    )
```

profile of v0, /device:TPU:0, one launch (start us, length us, event | category | flops | bytes accessed | tf_op | source)
XLA Modules:
  0.0 761.9 jit_solution(2233834308572963741)
XLA Ops:
  7.2 1.8 convert_reduce_fusion.5
  12.8 0.8 multiply_reduce_fusion.3
  14.5 1.3 copy-done.6
  15.8 1.1 fusion.87
  17.7 1.5 convolution_convert_fusion.5
  19.3 22.0 %all-reduce.14.cloned.1.call-done = bf16[512,768]{1,0:T(8,128)(2,1)} async-done(((bf16[512,768]{1,0:T(8,128)(2,1)}), bf16[512,768]{1,0:T(8,128)(2,1)}) %all-reduce.14.cloned.1.call-update) | async-done | bytes 786448 | tf_op jit(solution)/shard_map/psum | solution.py:146
  41.3 2.2 fusion.81
  43.5 1.8 convolution_convert_fusion.10
  45.7 1.3 copy-done.53
  48.2 0.8 multiply_reduce_fusion.2
  49.9 1.4 copy-done.7
  51.3 1.1 fusion.86
  53.2 1.5 convolution_convert_fusion.4
  57.0 18.3 %all-reduce.16.cloned.1.call-done = bf16[512,768]{1,0:T(8,128)(2,1)} async-done(((bf16[512,768]{1,0:T(8,128)(2,1)}), bf16[512,768]{1,0:T(8,128)(2,1)}) %all-reduce.16.cloned.1.call-update) | async-done | bytes 786448 | tf_op jit(solution)/shard_map/psum | solution.py:146
  75.3 2.6 multiply_reduce_fusion.5
  78.6 8.9 %multiply_convert_fusion.2 = (bf16[512,1536]{1,0:T(8,128)(2,1)}, f32[512,1536]{1,0:T(8,128)S(1)}, f32[512,1536]{1,0:T(8,128)S(1)}) fusion(bf16[768,1536]{1,0:T(8,128)(2,1)S(1)} %copy-done, f32[768]{0:T(1024)S(1)} %copy-done.56, f32[768]{0:T(1024)S(1)} %copy-done.55, f32[512]{0:T(512)S(1)} %add_rsqrt_fusion, f32[512]{0:T(512)S(1)} %get-tuple-element.163, ...), kind=kOutput, calls=%fused_computation.24 | convolution fusion | flops 1262223360 | bytes 11808768 | tf_op jit(solution)/shard_map/dot_general | solution.py:152
  87.5 2.2 add_convert_fusion
  89.7 2.3 convolution_convert_fusion
  92.1 21.4 %multiply_convert_fusion.3 = (bf16[512,1536]{1,0:T(8,128)(2,1)}, f32[512,1536]{1,0:T(8,128)S(1)}, f32[512,1536]{1,0:T(8,128)S(1)}) fusion(bf16[768,1536]{1,0:T(8,128)(2,1)S(1)} %copy-done, f32[768]{0:T(1024)S(1)} %copy-done.56, f32[768]{0:T(1024)S(1)} %copy-done.55, f32[512]{0:T(512)S(1)} %get-tuple-element.162, f32[512]{0:T(512)S(1)} %broadcast_multiply_fusion.10, ...), kind=kOutput, calls=%fused_computation.37 | convolution fusion | flops 1262223360 | bytes 11808768 | tf_op jit(solution)/shard_map/dot_general | solution.py:152
  113.5 2.2 add_convert_fusion.1
  115.7 1.1 copy-done.89
  116.8 2.3 convolution_convert_fusion.1
  119.3 1.3 copy-done.22
  120.6 4.1 convolution_convert_fusion.2
  124.7 2.3 convolution_convert_fusion.3
  127.0 14.0 %all-reduce.20.cloned.1.call-done = (bf16[512,768]{1,0:T(8,128)(2,1)}, bf16[512,768]{1,0:T(8,128)(2,1)}) async-done(((bf16[512,768]{1,0:T(8,128)(2,1)}, bf16[512,768]{1,0:T(8,128)(2,1)}), (bf16[512,768]{1,0:T(8,128)(2,1)}, bf16[512,768]{1,0:T(8,128)(2,1)})) %all-reduce.20.cloned.1.call-update) | async-done | bytes 1572880 | tf_op jit(solution)/shard_map/psum | solution.py:167
  141.0 3.7 fusion.74
  144.8 3.1 fusion.64
  149.1 1.7 fusion.93
  150.8 1.2 multiply_reduce_fusion
  152.0 1.4 multiply_convert_fusion
  153.4 1.5 fusion.89
  155.0 1.3 fusion.83
  156.9 1.7 fusion.90
  158.6 1.2 multiply_reduce_fusion.1
  159.8 1.3 multiply_convert_fusion.1
  161.2 1.6 fusion.88
  162.7 1.3 fusion.82
  164.0 1.2 copy.45
  165.2 2.0 copy.51
  167.1 1.8 copy.50
  169.0 1.9 copy.44
  170.8 2.3 convolution_bitcast_fusion
  173.1 1.6 add_convert_fusion.2
  175.7 1.5 add_convert_fusion.3
  178.2 2.2 fusion.116
  180.4 1.6 convolution_add_fusion.2
  182.2 1.6 convolution_bitcast_fusion.2
  183.9 0.9 convolution_bitcast_fusion.3
  184.7 1.0 copy-done.21
  188.4 2.2 maximum_add_fusion
  191.3 3.2 fusion.136
  194.5 4.2 convolution_add_fusion.1
  199.3 3.4 fusion.125
  202.7 3.8 convolution_add_fusion
  208.6 3.8 fusion.75
  212.4 77.1 %all-reduce.6 = (f32[768]{0:T(1024)S(1)}, f32[768]{0:T(1024)S(1)}, f32[768]{0:T(1024)S(1)}, f32[768]{0:T(1024)S(1)}) all-reduce(f32[768]{0:T(1024)S(1)} %add.239, f32[768]{0:T(1024)S(1)} %add.240, f32[768]{0:T(1024)S(1)} %add.241, f32[768]{0:T(1024)S(1)} %add.242), channel_id=6, replica_groups=mesh['dp'=16,'mp'=2] {'dp'}, use_global_device_ids=true, to_apply=%region_36.37.clone | all-reduce | flops 3072 | bytes 24576
  291.9 3.4 fusion.60
  295.3 1.3 pad_maximum_fusion.1
  296.6 1.9 pad_maximum_fusion
  298.5 33.4 %reduce-scatter.7.cloned.1.call-done = f32[384,48]{0,1:T(8,128)} async-done(((f32[384,768]{0,1:T(8,128)}), f32[384,48]{0,1:T(8,128)}) %reduce-scatter.7.cloned.1.call-update) | async-done | bytes 73744 | tf_op jit(solution)/shard_map/reduce_scatter | solution.py:106
  331.9 138.1 %reduce-scatter.5.cloned.1.call-done = f32[48,3,384]{2,0,1:T(8,128)} async-done(((f32[768,3,384]{2,0,1:T(8,128)}), f32[48,3,384]{2,0,1:T(8,128)}) %reduce-scatter.5.cloned.1.call-update) | async-done | bytes 221200 | tf_op jit(solution)/shard_map/reduce_scatter | solution.py:105
  469.9 142.4 %reduce-scatter.9.cloned.1.call-done = f32[48,1536]{1,0:T(8,128)} async-done(((f32[768,1536]{1,0:T(8,128)}), f32[48,1536]{1,0:T(8,128)}) %reduce-scatter.9.cloned.1.call-update) | async-done | bytes 294928 | tf_op jit(solution)/shard_map/reduce_scatter | solution.py:107
  612.3 142.3 %reduce-scatter.11.cloned.1.call-done = f32[1536,48]{0,1:T(8,128)} async-done(((f32[1536,768]{0,1:T(8,128)}), f32[1536,48]{0,1:T(8,128)}) %reduce-scatter.11.cloned.1.call-update) | async-done | bytes 294928 | tf_op jit(solution)/shard_map/reduce_scatter | solution.py:108
  (245 shorter events, 21.5 us)
Async XLA Ops:
  7.2 71.2 %copy-start = (bf16[768,1536]{1,0:T(8,128)(2,1)S(1)}, bf16[768,1536]{1,0:T(8,128)(2,1)}, u32[]{:S(2)}) copy-start(bf16[768,1536]{1,0:T(8,128)(2,1)} %param.15) | copy-start | bytes 7077892
  7.2 34.1 %all-reduce.14.cloned.1.call-start = ((), (), s32[]{:S(2)}) async-start(), calls=%async_computation.4 | async-start | bytes 1572864 | tf_op jit(solution)/shard_map/psum | solution.py:146
  7.2 2.0 copy-start.2
  13.7 2.2 copy-start.6
  15.8 1.9 copy-start.14
  19.2 56.0 %all-reduce.16.cloned.1.call-start = ((), (), s32[]{:S(2)}) async-start(), calls=%async_computation.5 | async-start | bytes 1572864 | tf_op jit(solution)/shard_map/psum | solution.py:146
  19.3 26.0 %copy-start.61 = (f32[512]{0:T(512)}, f32[512]{0:T(512)S(1)}, u32[]{:S(2)}) copy-start(f32[512]{0:T(512)S(1)} %broadcast_multiply_fusion.9) | copy-start | bytes 6148
  41.3 2.2 copy-start.3
  43.5 1.8 copy-start.68
  45.3 2.9 copy-start.40
  49.1 2.2 copy-start.7
  52.4 2.6 copy-start.85
  54.7 86.3 %all-reduce.20.cloned.1.call-start = ((), (), s32[]{:S(2)}) async-start(), calls=%async_computation.11 | async-start | bytes 3145728 | tf_op jit(solution)/shard_map/psum | solution.py:167
  56.9 87.8 %copy-start.70 = (f32[512]{0:T(512)}, f32[512]{0:T(512)S(1)}, u32[]{:S(2)}) copy-start(f32[512]{0:T(512)S(1)} %get-tuple-element.164) | copy-start | bytes 6148
  56.9 87.8 %copy-start.72 = (f32[512]{0:T(512)}, f32[512]{0:T(512)S(1)}, u32[]{:S(2)}) copy-start(f32[512]{0:T(512)S(1)} %get-tuple-element.165) | copy-start | bytes 6148
  56.9 87.8 %copy-start.74 = (f32[512]{0:T(512)}, f32[512]{0:T(512)S(1)}, u32[]{:S(2)}) copy-start(f32[512]{0:T(512)S(1)} %broadcast_multiply_fusion.10) | copy-start | bytes 6148
  75.3 2.7 copy-start.4
  75.3 2.7 copy-start.8
  77.9 14.2 %copy-start.76 = (f32[512]{0:T(512)}, f32[512]{0:T(512)S(1)}, u32[]{:S(2)}) copy-start(f32[512]{0:T(512)S(1)} %get-tuple-element.162) | copy-start | bytes 6148
  78.6 66.2 %copy-start.63 = (f32[512]{0:T(512)}, f32[512]{0:T(512)S(1)}, u32[]{:S(2)}) copy-start(f32[512]{0:T(512)S(1)} %add_rsqrt_fusion) | copy-start | bytes 6148
  78.6 8.9 %copy-start.16 = (bf16[2,512,768]{2,1,0:T(8,128)(2,1)S(1)}, bf16[2,512,768]{2,1,0:T(8,128)(2,1)}, u32[]{:S(2)}) copy-start(bf16[2,512,768]{2,1,0:T(8,128)(2,1)} %param.21) | copy-start | bytes 4718596
  78.6 8.9 %copy-start.86 = (bf16[1536,768]{1,0:T(8,128)(2,1)S(1)}, bf16[1536,768]{1,0:T(8,128)(2,1)}, u32[]{:S(2)}) copy-start(bf16[1536,768]{1,0:T(8,128)(2,1)} %param.16) | copy-start | bytes 7077892
  89.7 2.3 copy-start.28
  89.7 2.3 copy-start.12
  119.2 89.4 %all-reduce.18.cloned.1.call-start = ((), (), s32[]{:S(2)}) async-start(), calls=%async_computation.10 | async-start | bytes 6291456 | tf_op jit(solution)/shard_map/psum | solution.py:155
  120.6 4.1 copy-start.27
  120.6 4.1 copy-start.87
  124.6 16.4 %copy-start.5 = (bf16[2,512,768]{2,1,0:T(8,128)(2,1)S(1)}, bf16[2,512,768]{2,1,0:T(8,128)(2,1)}, u32[]{:S(2)}) copy-start(bf16[2,512,768]{2,1,0:T(8,128)(2,1)} %param.11) | copy-start | bytes 4718596
  124.6 16.4 %copy-start.13 = (bf16[512,768]{1,0:T(8,128)(2,1)S(1)}, bf16[512,768]{1,0:T(8,128)(2,1)}, u32[]{:S(2)}) copy-start(bf16[512,768]{1,0:T(8,128)(2,1)} %all-reduce.14.cloned.1.call-done) | copy-start | bytes 2359300
  124.6 16.4 %copy-start.77 = (f32[512]{0:T(512)S(1)}, f32[512]{0:T(512)}, u32[]{:S(2)}) copy-start(f32[512]{0:T(512)} %copy-done.76) | copy-start | bytes 6148
  141.0 8.1 %slice-start.2 = ((s8[4718592]{0:T(1024)(128)(4,1)}), s8[4194304]{0:T(1024)(128)(4,1)S(1)}, s32[]{:S(2)}) async-start(s8[4718592]{0:T(1024)(128)(4,1)} %bitcast.232), calls=%async_computation.14 | async-start | bytes 8388608
  144.8 3.2 copy-start.15
  144.8 4.3 slice-start.3
  147.9 8.4 %copy-start.9 = (f32[512,768]{1,0:T(8,128)}, f32[512,768]{1,0:T(8,128)S(1)}, u32[]{:S(2)}) copy-start(f32[512,768]{1,0:T(8,128)S(1)} %get-tuple-element.140) | copy-start | bytes 4718596
  150.8 6.1 slice-start
  152.0 4.8 slice-start.1
  165.2 9.6 %copy-start.42 = (bf16[1,384,384]{2,1,0:T(8,128)(2,1)}, bf16[1,384,384]{2,1,0:T(8,128)(2,1)S(1)}, u32[]{:S(2)}) copy-start(bf16[1,384,384]{2,1,0:T(8,128)(2,1)S(1)} %copy.45) | copy-start | bytes 884740
  170.8 2.3 copy-start.34
  170.8 2.3 copy-start.54
  177.2 154.6 %reduce-scatter.7.cloned.1.call-start = ((), (), s32[]{:S(2)}) async-start(), calls=%async_computation.7 | async-start | bytes 1253376 | tf_op jit(solution)/shard_map/reduce_scatter | solution.py:106
  178.2 2.2 copy-start.11
  178.2 2.2 copy-start.33
  180.4 1.7 copy-start.35
  182.1 287.8 %reduce-scatter.5.cloned.1.call-start = ((), (), s32[]{:S(2)}) async-start(), calls=%async_computation.6 | async-start | bytes 3760128 | tf_op jit(solution)/shard_map/reduce_scatter | solution.py:105
  183.8 1.9 copy-start.21
  183.8 2.0 copy-start.46
  183.9 2.2 copy-start.47
  190.7 3.8 copy-start.64
  190.7 421.7 %reduce-scatter.9.cloned.1.call-start = ((), (), s32[]{:S(2)}) async-start(), calls=%async_computation.8 | async-start | bytes 5013504 | tf_op jit(solution)/shard_map/reduce_scatter | solution.py:107
  191.3 3.2 copy-start.29
  198.7 4.0 copy-start.73
  198.7 555.9 %reduce-scatter.11.cloned.1.call-start = ((), (), s32[]{:S(2)}) async-start(), calls=%async_computation.9 | async-start | bytes 5013504 | tf_op jit(solution)/shard_map/reduce_scatter | solution.py:108
  199.3 3.4 copy-start.17
  199.3 3.4 copy-start.23
  206.6 1.9 copy-start.81
  206.6 1.9 copy-start.82
  206.6 1.9 copy-start.79
  206.6 1.9 copy-start.80
  206.6 2.0 copy-start.60
  206.6 2.0 copy-start.62
  206.6 2.0 copy-start.67
  206.6 2.0 copy-start.69
  291.8 3.4 copy-start.24
  296.6 458.0 %copy-start.1 = (bf16[768,1536]{1,0:T(8,128)(2,1)S(1)}, bf16[768,1536]{1,0:T(8,128)(2,1)}, u32[]{:S(2)}) copy-start(bf16[768,1536]{1,0:T(8,128)(2,1)} %param.15) | copy-start | bytes 7077892
  (38 other events, 46.4 us)
Sparse Core Ops, SparseCore 0:
  19.3 21.8 all-reduce.13
  54.8 20.3 all-reduce.15
  119.3 21.6 all-reduce.19
  177.4 24.5 all-reduce.17
  207.1 124.6 reduce-scatter.6
  337.4 132.4 reduce-scatter.4
  475.7 136.6 reduce-scatter.8
  618.9 135.6 reduce-scatter.10
where the time goes:
time: 771 us; the launch traced here: 762 us
  waiting for transfers between devices  511 us (66%)
  matrix products  97.8 us (13%)
  blocking collectives  77.1 us (10%)
  other arithmetic  31.8 us (4%)
  local copies, waits for them, and re-layouts  26.1 us (3%)
  between operations  17.7 us (2%)
    reduce_scatter x1, waiting for transfers between devices, reduce_total(): lax.psum_scatter(grads[2], 'dp', scatter_dimension=0, tiled=True)  142 us
    reduce_scatter x1, waiting for transfers between devices, reduce_total(): lax.psum_scatter(grads[3], 'dp', scatter_dimension=1, tiled=True)  142 us
    reduce_scatter x1, waiting for transfers between devices, reduce_total(): lax.psum_scatter(grads[0], 'dp', scatter_dimension=0, tiled=True)  138 us
    unnamed x1, blocking collectives  77.1 us
    psum x2, waiting for transfers between devices, per_device(): lax.psum(jnp.dot(heads_out, w_out, preferred_element_type=jnp.float32).as...  40.3 us
    reduce_scatter x1, waiting for transfers between devices, reduce_total(): lax.psum_scatter(grads[1], 'dp', scatter_dimension=1, tiled=True)  33.4 us
    dot_general x2, matrix products, per_device(): lifted = jnp.dot(normed_two, w_up, preferred_element_type=jnp.float32)  30.3 us
    unnamed x193, local copies, waits for them, and re-layouts  18.6 us
  transfers between devices with their start and end apart: 8, of which 7 were waited for; matrix products, arithmetic and copies ran while one was open for 6% of the time, Pallas kernels for 0%

commit v1 on v0

v1 whole, which is shorter than its diff:
```python
import math

import jax
import jax.numpy as jnp
from jax import lax
from jax.experimental import pallas as pl
from jax.experimental.pallas import tpu as pltpu
from jax.sharding import PartitionSpec as P

HD = 64
CTX = 384
EPS = 1e-05
BF = jnp.bfloat16
F32 = jnp.float32
MESH = pl.DeviceIdType.MESH
PAIR = 2 * HD
RB = 256


def nn(a, b):
    return lax.dot_general(a, b, (((1,), (0,)), ((), ())), preferred_element_type=F32)


def nt(a, b):
    return lax.dot_general(a, b, (((1,), (1,)), ((), ())), preferred_element_type=F32)


def unit_rows(rows):
    centre = jnp.mean(rows, axis=-1, keepdims=True)
    centred = rows - centre
    inverse = lax.rsqrt(jnp.mean(centred * centred, axis=-1, keepdims=True) + EPS)
    return centred * inverse, inverse


def norm_backward(grad, unit, inverse, gain):
    u = grad * gain
    first = jnp.mean(u, axis=-1, keepdims=True)
    second = jnp.mean(u * unit, axis=-1, keepdims=True)
    return inverse * (u - first - unit * second)


class Plan:
    def __init__(self, tables, seq, width, heads, hidden, dp):
        self.tables, self.seq, self.width, self.heads, self.hidden, self.dp = tables, seq, width, heads, hidden, dp
        self.rows = tables * seq
        self.share = width // dp
        self.fused = dp == 16 and self.share % 16 == 0
        self.step = 512 if hidden % 512 == 0 else 256
        chunks = []
        steps = hidden // self.step
        for c in range(steps):
            chunks.append(("down", c * self.step, self.step, "x"))
            chunks.append(("up", hidden + c * self.step, self.step, "y"))
        at = 2 * hidden
        for name, kind in (("out", "x"), ("q", "y"), ("k", "x"), ("v", "y")):
            chunks.append((name, at, heads, kind))
            at += heads
        chunks.append(("vec", at, 128, "x"))
        self.chunks = chunks
        self.columns = at + 128
        self.first = {name: start for name, start, _, _ in reversed(chunks)}


def layer_kernel(
    plan,
    counts_ref, x_hbm, wqkv_hbm, wout_hbm, wup_hbm, wdown_hbm, gains_hbm, cot_hbm,
    out_hbm, gin_hbm, red_hbm,
    x, wqkv, wout, wup, wdown, gains, gl,
    nrm, q, k, v, prob, ho, resid, n2, n2t, glt, act, glf, vec,
    xs, xr_a, xr_b, ms, mr,
    g, r1, r2, r3, red,
    in_sem, out_sem, xsend, xrecv, s1, q1, s2, q2, s3, q3,
):
    T, S, D, H, FF = plan.tables, plan.seq, plan.width, plan.heads, plan.hidden
    R = plan.rows
    pairs = H // PAIR
    dp = lax.axis_index("dp")
    mp = lax.axis_index("mp")
    xx, yy, zz = lax.rem(dp, 2), lax.rem(lax.div(dp, 2), 2), lax.div(dp, 4)
    partner = (dp, 1 - mp)

    def chip(z, y, x_):
        return (z * 4 + y * 2 + x_, mp)

    x_peer, y_peer = chip(zz, yy, 1 - xx), chip(zz, 1 - yy, xx)
    z_peers = [chip(lax.rem(zz + d, 4), yy, xx) for d in (1, 2, 3)]
    peers = [partner] + ([x_peer, y_peer] + z_peers if plan.fused else [])

    loads = [
        pltpu.make_async_copy(a, b, in_sem.at[i])
        for i, (a, b) in enumerate(
            ((x_hbm, x), (gains_hbm, gains), (wqkv_hbm, wqkv), (wout_hbm, wout), (cot_hbm, gl), (wup_hbm, wup), (wdown_hbm, wdown))
        )
    ]
    for c in loads:
        c.start()
    barrier = pltpu.get_barrier_semaphore()
    for n in peers:
        pl.semaphore_signal(barrier, inc=1, device_id=n, device_id_type=MESH)
    pl.semaphore_wait(barrier, len(peers))

    def remote(src, dst, ss, rs, dev):
        return pltpu.make_async_remote_copy(src, dst, ss, rs, device_id=dev, device_id_type=MESH)

    def swap(i, t, src, dst):
        rows = pl.ds(t * S, S)
        return remote(src.at[rows], dst.at[rows], xsend.at[i, t], xrecv.at[i, t], partner)

    def stages(i):
        _, c0, cw, kind = plan.chunks[i]
        cs = pl.ds(c0, cw)
        isx = kind == "x"
        other, mine = (1 - yy, yy) if isx else (1 - xx, xx)
        c1 = remote(
            g.at[:, :, 1 - xx, :, cs] if isx else g.at[:, 1 - yy, :, :, cs],
            r1.at[:, :, :, cs], s1.at[i], q1.at[i], x_peer if isx else y_peer,
        )
        c2 = remote(r1.at[:, other, :, cs], r2.at[:, :, cs], s2.at[i], q2.at[i], y_peer if isx else x_peer)
        c3 = [
            remote(r2.at[lax.rem(zz + d, 4), :, cs], r3.at[d - 1, :, cs], s3.at[i, d - 1], q3.at[i, d - 1], z_peers[d - 1])
            for d in (1, 2, 3)
        ]

        def add_one():
            c1.wait_recv()

            def part(p):
                for z in range(4):
                    own = g[z, p, xx, :, cs] if isx else g[z, yy, p, :, cs]
                    r1[z, p, :, cs] = (own.astype(F32) + r1[z, p, :, cs].astype(F32)).astype(BF)

            part(other)
            c2.start()
            part(mine)

        def add_two():
            c2.wait_recv()
            for d in (2, 3, 1, 0):
                z = lax.rem(zz + d, 4)
                r2[z, :, cs] = (r1[z, mine, :, cs].astype(F32) + r2[z, :, cs].astype(F32)).astype(BF)
                if d:
                    c3[d - 1].start()

        def add_three():
            for c in c3:
                c.wait_recv()
            total = r2[zz, :, cs].astype(F32)
            for d in range(3):
                total = total + r3[d, :, cs].astype(F32)
            red[:, cs] = total

        def drain():
            for c in (c1, c2, *c3):
                c.wait_send()

        return c1.start, add_one, add_two, add_three, drain

    ready = set()
    events = []
    if plan.fused:
        prog = [stages(i) for i in range(len(plan.chunks))]
        count = len(prog)
        window, lag = 2, 1
        for i in range(min(window, count)):
            events.append((i, prog[i][0]))
        for t in range(count + 2 * lag):
            if t < count:
                events.append((t, prog[t][1]))
                if t + window < count:
                    events.append((t + window, prog[t + window][0]))
            if 0 <= t - lag < count:
                events.append((t - lag, prog[t - lag][2]))
            if 0 <= t - 2 * lag < count:
                events.append((t - 2 * lag, prog[t - 2 * lag][3]))

    def service(n):
        while n > 0 and events and events[0][0] in ready:
            events.pop(0)[1]()
            n -= 1

    def made(name, i=0):
        for j, c in enumerate(plan.chunks):
            if c[0] == name:
                if i == 0:
                    ready.add(j)
                    return
                i -= 1

    def put(c0, cw, rows768):
        cs = pl.ds(c0, cw)
        if plan.fused:
            g[:, :, :, :, cs] = rows768.astype(BF).reshape(4, 2, 2, plan.share, cw)
        else:
            g[:, cs] = rows768.astype(BF)

    def blocks(n, body):
        def step(i, carry):
            body(i)
            return carry

        lax.fori_loop(0, n, step, 0)

    def rows_of(b):
        return pl.ds(pl.multiple_of(b * RB, RB), RB)

    loads[0].wait()
    loads[1].wait()
    g1, b1, g2, b2 = (gains[i : i + 1, :] for i in range(4))

    def first_norm(b):
        rs = rows_of(b)
        unit, _ = unit_rows(x[rs, :].astype(F32))
        nrm[rs, :] = (unit * g1 + b1).astype(BF)

    blocks(R // RB, first_norm)
    loads[2].wait()

    def project(t):
        all_rows = pl.ds(pl.multiple_of(t * S, S), S)
        context = pl.ds(pl.multiple_of(t * S, S), CTX)
        q[all_rows, :] = nn(nrm[all_rows, :], wqkv[:, 0:H]).astype(BF)
        k[context, :] = nn(nrm[context, :], wqkv[:, H : 2 * H]).astype(BF)
        v[context, :] = nn(nrm[context, :], wqkv[:, 2 * H : 3 * H]).astype(BF)

    blocks(T, project)

    scale = 1.0 / math.sqrt(HD)
    low_lane = lax.broadcasted_iota(jnp.int32, (CTX, PAIR), 1) < HD
    low_row = lax.broadcasted_iota(jnp.int32, (PAIR, CTX), 0) < HD

    def stacked(a):
        zero = jnp.zeros_like(a)
        return jnp.concatenate([jnp.where(low_lane, a, zero), jnp.where(low_lane, zero, a)], axis=0)

    def beside(a):
        at = a.T
        zero = jnp.zeros_like(at)
        return jnp.concatenate([jnp.where(low_row, at, zero), jnp.where(low_row, zero, at)], axis=1)

    def merged(a):
        return jnp.where(low_lane, a[:CTX], a[CTX:])

    def attend(t, h):
        rows = pl.ds(pl.multiple_of(t * S, S), S)
        context = pl.ds(pl.multiple_of(t * S, S), CTX)
        cols = pl.ds(pl.multiple_of(h * PAIR, PAIR), PAIR)
        slot = t * pairs + h
        scores = nt(stacked(k[context, cols]), q[rows, cols])
        halves = []
        for i in range(2):
            s = scores[i * CTX : (i + 1) * CTX]
            e = jnp.exp((s - jnp.max(s, axis=0, keepdims=True)) * scale)
            p = e * (1.0 / jnp.sum(e, axis=0, keepdims=True))
            prob[slot, i * CTX : (i + 1) * CTX, :] = p
            halves.append(p.astype(BF))
        out_t = nn(beside(v[context, cols]), jnp.concatenate(halves, axis=0))
        ho[rows, cols] = out_t.T.astype(BF)

    loads[3].wait()
    for t in range(T):
        blocks(pairs, lambda h, t=t: attend(t, h))
        rows = pl.ds(t * S, S)
        xs[rows, :] = nn(ho[rows, :], wout[...]).astype(BF)
        swap(0, t, xs, xr_a).start()

    loads[4].wait()

    def mask(b):
        rs = rows_of(b)
        pos = lax.broadcasted_iota(jnp.int32, (RB, 1), 0) + lax.rem(b * RB, S)
        live = pos < CTX + counts_ref[lax.div(b * RB, S)]
        kept = jnp.where(live, gl[rs, :].astype(F32), 0.0).astype(BF)
        gl[rs, :] = kept
        glt[:, rs] = kept.T

    blocks(R // RB, mask)

    def second_norm(b):
        rs = rows_of(b)
        r = x[rs, :].astype(F32) + (xs[rs, :].astype(F32) + xr_a[rs, :].astype(F32))
        resid[rs, :] = r
        unit, _ = unit_rows(r)
        low = (unit * g2 + b2).astype(BF)
        n2[rs, :] = low
        n2t[:, rs] = low.T

    per = S // RB
    for t in range(T):
        swap(0, t, xs, xr_a).wait_recv()
        blocks(per, lambda i, t=t: second_norm(t * per + i))
    loads[5].wait()
    loads[6].wait()

    def feed(c0, cw):
        cs = pl.ds(c0, cw)

        def body(b):
            rs = rows_of(b)
            lifted = nn(n2[rs, :], wup[:, cs])
            half = 0.5 + 0.5 * lax.erf(lifted * (1.0 / math.sqrt(2.0)))
            act[rs, cs] = (lifted * half).astype(BF)
            slope = half + lifted * (jnp.exp(-0.5 * lifted * lifted) * (1.0 / math.sqrt(2.0 * math.pi)))
            glf[rs, cs] = (slope * nt(gl[rs, :], wdown[cs, :])).astype(BF)

        blocks(R // RB, body)

    def grad_tiles(c0, left, right, r0, cw):
        tile = 256 if cw % 256 == 0 else 128

        def body(j):
            off = pl.multiple_of(j * tile, tile)
            put(c0 + off, tile, nn(left, right[:, pl.ds(r0 + off, tile)]))

        blocks(cw // tile, body)

    steps = FF // plan.step
    for c in range(steps):
        c0 = c * plan.step
        feed(c0, plan.step)
        grad_tiles(c0, glt[...], act, c0, plan.step)
        made("down", c)
        service(1 if c == 0 else 2)
        grad_tiles(FF + c0, n2t[...], glf, c0, plan.step)
        made("up", c)
        service(1 if c == 0 else 2)

    swap_send = lambda i, t, src, dst: swap(i, t, src, dst).wait_send()
    for t in range(T):
        swap_send(0, t, xs, xr_a)
    for t in range(T):
        rows = pl.ds(t * S, S)

        def body(j, rows=rows):
            cs = pl.ds(pl.multiple_of(j * 256, 256), 256)
            xs[rows, cs] = nt(glf[rows, :], wup[cs, :]).astype(BF)
            ms[rows, cs] = nn(act[rows, :], wdown[:, cs]).astype(BF)

        blocks(D // 256, body)
        swap(1, t, xs, xr_b).start()
        swap(2, t, ms, mr).start()
        service(2)

    def output(b):
        rs = rows_of(b)
        pos = lax.broadcasted_iota(jnp.int32, (RB, 1), 0) + lax.rem(b * RB, S)
        live = pos < CTX + counts_ref[lax.div(b * RB, S)]
        total = resid[rs, :] + (ms[rs, :].astype(F32) + mr[rs, :].astype(F32))
        n2[rs, :] = jnp.where(live, total, 0.0).astype(BF)

    vec[...] = jnp.zeros_like(vec)

    def second_back(b):
        rs = rows_of(b)
        grad = xs[rs, :].astype(F32) + xr_b[rs, :].astype(F32)
        unit, inverse = unit_rows(resid[rs, :])
        vec[2:3, :] += jnp.sum(grad * unit, axis=0, keepdims=True)
        vec[3:4, :] += jnp.sum(grad, axis=0, keepdims=True)
        total = gl[rs, :].astype(F32) + norm_backward(grad, unit, inverse, g2)
        resid[rs, :] = total
        low = total.astype(BF)
        gl[rs, :] = low
        n2t[:, rs] = low.T

    for t in range(T):
        swap(2, t, ms, mr).wait_recv()
        blocks(per, lambda i, t=t: output(t * per + i))
        swap(1, t, xs, xr_b).wait_recv()
        blocks(per, lambda i, t=t: second_back(t * per + i))
        service(2)
    store_out = pltpu.make_async_copy(n2, out_hbm, out_sem.at[0])
    store_out.start()

    grad_tiles(plan.first["out"], n2t[...], ho, 0, H)
    made("out")
    service(2)

    gh, gq, gk, gv = 0, H, 2 * H, 3 * H

    def heads_back(t):
        rows = pl.ds(pl.multiple_of(t * S, S), S)
        act[rows, gh : gh + H] = nt(gl[rows, :], wout[...]).astype(BF)

    blocks(T, heads_back)
    service(2)

    def attend_back(t, h):
        rows = pl.ds(pl.multiple_of(t * S, S), S)
        context = pl.ds(pl.multiple_of(t * S, S), CTX)
        off = pl.multiple_of(h * PAIR, PAIR)
        cols = pl.ds(off, PAIR)
        slot = t * pairs + h
        grad2 = act[rows, pl.ds(gh + off, PAIR)]
        back = nt(stacked(v[context, cols]), grad2)
        low_p, low_s = [], []
        for i in range(2):
            p = prob[slot, i * CTX : (i + 1) * CTX, :]
            b = back[i * CTX : (i + 1) * CTX]
            low_p.append(p.astype(BF))
            low_s.append((p * (b - jnp.sum(p * b, axis=0, keepdims=True))).astype(BF))
        low_p = jnp.concatenate(low_p, axis=0)
        low_s = jnp.concatenate(low_s, axis=0)
        act[rows, pl.ds(gq + off, PAIR)] = (nn(beside(k[context, cols]), low_s).T * scale).astype(BF)
        act[context, pl.ds(gk + off, PAIR)] = (merged(nn(low_s, q[rows, cols])) * scale).astype(BF)
        act[context, pl.ds(gv + off, PAIR)] = merged(nn(low_p, grad2)).astype(BF)

    for t in range(T):
        blocks(pairs, lambda h, t=t: attend_back(t, h))
        service(2)

    def transpose_normed(b):
        rs = rows_of(b)
        glt[:, rs] = nrm[rs, :].T

    blocks(R // RB, transpose_normed)
    grad_tiles(plan.first["q"], glt[...], act, gq, H)
    made("q")
    service(2)

    def context_tiles(c0, r0):
        def body(j):
            off = pl.multiple_of(j * 128, 128)
            total = None
            for t in range(T):
                part = nn(glt[:, t * S : t * S + CTX], act[t * S : t * S + CTX, pl.ds(r0 + off, 128)])
                total = part if total is None else total + part
            put(c0 + off, 128, total)

        blocks(H // 128, body)

    context_tiles(plan.first["k"], gk)
    made("k")
    service(2)
    context_tiles(plan.first["v"], gv)
    made("v")
    service(2)

    for t in range(T):
        swap_send(1, t, xs, xr_b)
    for t in range(T):
        rows = pl.ds(t * S, S)

        def body(j, t=t, rows=rows):
            cs = pl.ds(pl.multiple_of(j * 256, 256), 256)
            part = nt(act[rows, gq : gq + H], wqkv[cs, 0:H])
            ctx = slice(t * S, t * S + CTX)
            extra = nt(act[ctx, gk : gk + 2 * H], wqkv[cs, H : 3 * H])
            xs[t * S : t * S + CTX, cs] = (part[:CTX] + extra).astype(BF)
            xs[t * S + CTX : (t + 1) * S, cs] = part[CTX:].astype(BF)

        blocks(D // 256, body)
        swap(3, t, xs, xr_a).start()
        service(1)

    def first_back(b):
        rs = rows_of(b)
        grad = xs[rs, :].astype(F32) + xr_a[rs, :].astype(F32)
        unit, inverse = unit_rows(x[rs, :].astype(F32))
        vec[0:1, :] += jnp.sum(grad * unit, axis=0, keepdims=True)
        vec[1:2, :] += jnp.sum(grad, axis=0, keepdims=True)
        resid[rs, :] = resid[rs, :] + norm_backward(grad, unit, inverse, g1)

    for t in range(T):
        swap(3, t, xs, xr_a).wait_recv()
        blocks(per, lambda i, t=t: first_back(t * per + i))
    store_gin = pltpu.make_async_copy(resid, gin_hbm, out_sem.at[1])
    store_gin.start()
    put(plan.first["vec"], 128, jnp.concatenate([vec[...], jnp.zeros((128 - vec.shape[0], D), F32)], axis=0).T)
    made("vec")
    service(1000)
    assert not events

    if plan.fused:
        store_red = pltpu.make_async_copy(red, red_hbm, out_sem.at[2])
    else:
        store_red = pltpu.make_async_copy(g, red_hbm, out_sem.at[2])
    store_red.start()
    if plan.fused:
        for p in prog:
            p[4]()
    for t in range(T):
        swap_send(2, t, ms, mr)
        swap_send(3, t, xs, xr_a)
    store_out.wait()
    store_gin.wait()
    store_red.wait()


def run_layer(plan, counts, x, wqkv, wout, wup, wdown, gains, cot):
    R, D, H, FF, W = plan.rows, plan.width, plan.heads, plan.hidden, plan.columns
    V = pltpu.VMEM
    DMA = pltpu.SemaphoreType.DMA
    n = len(plan.chunks)
    if plan.fused:
        gshape, redshape, share = (4, 2, 2, plan.share, W), (plan.share, W), plan.share
        comm = [V((4, 2, share, W), BF), V((4, share, W), BF), V((3, share, W), BF), V(redshape, F32)]
        red_type = jax.ShapeDtypeStruct(redshape, F32)
    else:
        gshape = (D, W)
        comm = [V((8, 128), F32)] * 4
        red_type = jax.ShapeDtypeStruct(gshape, BF)
    scratch = [
        V((R, D), BF), V((D, 3 * H), BF), V((H, D), BF), V((D, FF), BF), V((FF, D), BF), V((4, D), F32), V((R, D), BF),
        V((R, D), BF), V((R, H), BF), V((R, H), BF), V((R, H), BF),
        V((plan.tables * (H // PAIR), 2 * CTX, plan.seq), F32), V((R, H), BF), V((R, D), F32), V((R, D), BF),
        V((D, R), BF), V((D, R), BF), V((R, FF), BF), V((R, FF), BF), V((8, D), F32),
        V((R, D), BF), V((R, D), BF), V((R, D), BF), V((R, D), BF), V((R, D), BF),
        V(gshape, BF), *comm,
        DMA((7,)), DMA((3,)), DMA((4, plan.tables)), DMA((4, plan.tables)),
        DMA((n,)), DMA((n,)), DMA((n,)), DMA((n,)), DMA((n, 3)), DMA((n, 3)),
    ]
    hbm = pl.BlockSpec(memory_space=pl.ANY)

    def kernel(*refs):
        layer_kernel(plan, *refs)

    return pl.pallas_call(
        kernel,
        out_shape=(jax.ShapeDtypeStruct((R, D), BF), jax.ShapeDtypeStruct((R, D), F32), red_type),
        in_specs=[pl.BlockSpec(memory_space=pltpu.SMEM)] + [hbm] * 7,
        out_specs=(hbm,) * 3,
        scratch_shapes=scratch,
        compiler_params=pltpu.CompilerParams(collective_id=0, has_side_effects=True, vmem_limit_bytes=67043328),
        name="layer",
    )(counts, x, wqkv, wout, wup, wdown, gains, cot)


def per_device(dp, inputs, counts, w_qkv, w_out, w_up, w_down, gain_one, shift_one, gain_two, shift_two, cotangent):
    tables, seq, width = inputs.shape
    heads, hidden = w_out.shape[0], w_up.shape[1]
    plan = Plan(tables, seq, width, heads, hidden, dp)
    rows = tables * seq
    out, gin, red = run_layer(
        plan,
        counts,
        inputs.reshape(rows, width),
        w_qkv.reshape(width, 3 * heads),
        w_out,
        w_up,
        w_down,
        jnp.stack([gain_one, shift_one, gain_two, shift_two]),
        cotangent.reshape(rows, width),
    )
    if not plan.fused:
        red = lax.psum_scatter(red.astype(F32), "dp", scatter_dimension=0, tiled=True)
    at = 2 * hidden
    vec = red[:, at + 4 * heads : at + 4 * heads + 4]
    return (
        out.reshape(inputs.shape),
        gin.reshape(inputs.shape),
        red[:, at + heads : at + 4 * heads].reshape(-1, 3, heads),
        red[:, at : at + heads].T,
        red[:, hidden:at],
        red[:, :hidden].T,
        vec[:, 0],
        vec[:, 1],
        vec[:, 2],
        vec[:, 3],
    )


def solution(mesh):
    dp = mesh.shape["dp"]
    in_specs = (
        P("dp", None, None), P("dp"), P(None, None, "mp"), P("mp", None), P(None, "mp"), P("mp", None),
        P(), P(), P(), P(), P("dp", None, None),
    )
    out_specs = (
        P("dp", None, None), P("dp", None, None), P("dp", None, "mp"), P("mp", "dp"), P("dp", "mp"), P("mp", "dp"),
        P("dp"), P("dp"), P("dp"), P("dp"),
    )

    def step(*args):
        return per_device(dp, *args)

    return jax.shard_map(step, mesh=mesh, in_specs=in_specs, out_specs=out_specs, check_vma=False)
```

time: 771 us -> 127 us (0.16); the launches traced: 762 us -> 127 us
  waiting for transfers between devices: 511 us -> 0 us
  Pallas kernels: 0 us -> 110 us
  matrix products: 97.8 us -> 0 us
  blocking collectives: 77.1 us -> 0 us
  other arithmetic: 31.8 us -> 0.62 us
  between operations: 17.7 us -> 0.76 us
  local copies, waits for them, and re-layouts: 26.1 us -> 14.8 us
    reduce_scatter x4 -> x0, waiting for transfers between devices: 456 us -> none  [the longest x1 142 us: reduce_total(): lax.psum_scatter(grads[2], 'dp', scatter_dimension=0, tiled=True)]
    pallas_call x0 -> x1, Pallas kernels: none -> 110 us  [run_layer(): pl.pallas_call(kernel, out_shape=(jax.ShapeDtypeStruct((R, D), BF), jax.S...]
    dot_general x42 -> x0, matrix products: 97.8 us -> none  [the longest x2 30.3 us: per_device(): lifted = jnp.dot(normed_two, w_up, preferred_element_type=jnp.float32)]
    unnamed x1 -> x0, blocking collectives: 77.1 us -> none
    psum x4 -> x0, waiting for transfers between devices: 54.3 us -> none  [the longest x2 40.3 us: per_device(): lax.psum(jnp.dot(heads_out, w_out, preferred_element_type=jnp.float32).as...]
    reduce_sum x9 -> x0, other arithmetic: 16.5 us -> none  [the longest x2 4.04 us: layer_norm(): centre = jnp.mean(row_data, axis=-1, keepdims=True)]
    unnamed x193 -> x15, local copies, waits for them, and re-layouts: 18.6 us -> 5.47 us
  transfers between devices with their start and end apart: 8 -> 0, of which waited for: 7 -> 0; matrix products, arithmetic and copies ran while one was open for 6% -> 0% of each run, Pallas kernels for 0% -> 0%
where the time goes in v1:
time: 127 us
  Pallas kernels  110 us (87%)
  local copies, waits for them, and re-layouts  14.8 us (12%)
    pallas_call x1, Pallas kernels, run_layer(): pl.pallas_call(kernel, out_shape=(jax.ShapeDtypeStruct((R, D), BF), jax.S...  110 us
    unnamed x15, local copies, waits for them, and re-layouts  5.47 us

profile of v1, /device:TPU:0, one launch (start us, length us, event | category | flops | bytes accessed | tf_op | source)
XLA Modules:
  0.0 126.5 jit_solution(10495612105218597201)
XLA Ops:
  0.6 2.6 %copy.23 = bf16[768,3,384]{0,2,1:T(8,128)(2,1)S(1)} copy(bf16[768,3,384]{2,0,1:T(8,128)(2,1)} %param.13) | data formatting | bytes 3538944 | tf_op args[2]
  3.3 0.0 copy-start.2
  3.3 0.0 copy-start.3
  3.3 0.0 copy-start.4
  3.3 0.0 copy-start.5
  3.3 2.2 %copy.24.refs_2_ = bf16[768,1152]{1,0:T(8,128)(2,1)} copy(bf16[768,1152]{0,1:T(8,128)(2,1)S(1)} %bitcast.13) | data formatting | bytes 3538944 | tf_op jit(solution)/shard_map/reshape | solution.py:536
  5.5 0.0 copy-done.2
  5.5 0.0 copy-done.3
  5.6 0.0 copy-done.4
  5.6 0.0 copy-done.5
  5.6 0.6 pad_maximum_fusion.refs_6_
  6.2 110.4 %layer.1 = (bf16[1024,768]{1,0:T(8,128)(2,1)}, f32[1024,768]{1,0:T(8,128)}, f32[48,4736]{1,0:T(8,128)}) custom-call(s32[2]{0:T(128)} %refs_0_.1, bf16[1024,768]{1,0:T(8,128)(2,1)} %bitcast.16, bf16[768,1152]{1,0:T(8,128)(2,1)} %copy.24.refs_2_, bf16[384,768]{1,0:T(8,128)(2,1)} %refs_3_.1, bf16[768,1536]{1,0:T(8,128)(2,1)} %refs_4_.1, ...), custom_call_target="tpu_custom_call" | custom-call | tf_op jit(solution)/shard_map/layer/pallas_call | solution.py:516
  116.6 0.0 copy-start.1
  116.6 1.7 %slice_reduce_fusion = (f32[48]{0:T(128)}, f32[48]{0:T(128)}, f32[48]{0:T(128)}, f32[48]{0:T(128)}) fusion(f32[48,4736]{1,0:T(8,128)} %get-tuple-element.15), kind=kLoop, calls=%fused_computation.3 | loop fusion | bytes 1536 | tf_op jit(solution)/shard_map/slice | solution.py:557
  118.3 1.9 %slice_bitcast_fusion = (f32[1536,48]{0,1:T(8,128)}, f32[48,1536]{1,0:T(8,128)}) fusion(f32[48,4736]{1,0:T(8,128)} %get-tuple-element.15), kind=kLoop, calls=%fused_computation | loop fusion | bytes 1179648 | tf_op jit(solution)/shard_map/transpose | solution.py:553
  120.2 0.9 slice.29
  121.2 0.0 copy-start
  121.2 0.7 copy.28
  121.9 1.8 %slice_bitcast_fusion.1 = f32[384,48]{0,1:T(8,128)} fusion(f32[48,4736]{1,0:T(8,128)} %get-tuple-element.15), kind=kLoop, calls=%fused_computation.2 | loop fusion | bytes 147456 | tf_op jit(solution)/shard_map/transpose | solution.py:551
  123.7 0.0 copy-done.1
  123.7 1.1 copy.31
  124.9 0.0 copy-done
  124.9 1.7 %copy.32 = f32[2,512,768]{2,1,0:T(8,128)} copy(f32[2,512,768]{2,1,0:T(8,128)S(1)} %bitcast.14) | data formatting | bytes 6291456
  (4 shorter events, 0.0 us)
Async XLA Ops:
  3.3 2.3 %copy-start.2 = (f32[768]{0:T(1024)S(1)}, f32[768]{0:T(1024)}, u32[]{:S(2)}) copy-start(f32[768]{0:T(1024)} %param.17) | copy-start | bytes 9220
  3.3 2.3 %copy-start.3 = (f32[768]{0:T(1024)S(1)}, f32[768]{0:T(1024)}, u32[]{:S(2)}) copy-start(f32[768]{0:T(1024)} %param.18) | copy-start | bytes 9220
  3.3 2.3 %copy-start.4 = (f32[768]{0:T(1024)S(1)}, f32[768]{0:T(1024)}, u32[]{:S(2)}) copy-start(f32[768]{0:T(1024)} %param.19) | copy-start | bytes 9220
  3.3 2.3 %copy-start.5 = (f32[768]{0:T(1024)S(1)}, f32[768]{0:T(1024)}, u32[]{:S(2)}) copy-start(f32[768]{0:T(1024)} %param.20) | copy-start | bytes 9220
  116.6 7.1 %copy-start.1 = (bf16[1024,768]{1,0:T(8,128)(2,1)S(1)}, bf16[1024,768]{1,0:T(8,128)(2,1)}, u32[]{:S(2)}) copy-start(bf16[1024,768]{1,0:T(8,128)(2,1)} %get-tuple-element.13) | copy-start | bytes 4718596
  121.2 3.7 %copy-start = (f32[1024,768]{1,0:T(8,128)S(1)}, f32[1024,768]{1,0:T(8,128)}, u32[]{:S(2)}) copy-start(f32[1024,768]{1,0:T(8,128)} %get-tuple-element.14) | copy-start | bytes 9437188

commit v2 on v1

v2 whole, which is shorter than its diff:
```python
import math

import jax
import jax.numpy as jnp
from jax import lax
from jax.experimental import pallas as pl
from jax.experimental.pallas import tpu as pltpu
from jax.sharding import PartitionSpec as P

HD = 64
CTX = 384
EPS = 1e-05
BF = jnp.bfloat16
F32 = jnp.float32
MESH = pl.DeviceIdType.MESH
PAIR = 2 * HD
RB = 256


def nn(a, b):
    return lax.dot_general(a, b, (((1,), (0,)), ((), ())), preferred_element_type=F32)


def nt(a, b):
    return lax.dot_general(a, b, (((1,), (1,)), ((), ())), preferred_element_type=F32)


def unit_rows(rows):
    centre = jnp.mean(rows, axis=-1, keepdims=True)
    centred = rows - centre
    inverse = lax.rsqrt(jnp.mean(centred * centred, axis=-1, keepdims=True) + EPS)
    return centred * inverse, inverse


def norm_backward(grad, unit, inverse, gain):
    u = grad * gain
    first = jnp.mean(u, axis=-1, keepdims=True)
    second = jnp.mean(u * unit, axis=-1, keepdims=True)
    return inverse * (u - first - unit * second)


HOPS = ('x', 'y', 'x', 'y', 'zy', 'x', 'x', 'x', 'y', 'zy', 'zy', 'y', 'x', 'x', 'y', 'y', 'x', 'y', 'y', 'x', 'y', 'x', 'y', 'x', 'x')
ORDER = ((0, 0), (1, 0), (2, 0), (3, 0), (4, 0), (5, 0), (0, 1), (1, 1), (2, 1), (8, 0), (3, 1), (4, 1), (9, 0), (0, 2), (6, 0), (5, 1), (2, 2), (11, 0), (1, 2), (7, 0), (3, 2), (8, 1), (9, 1), (4, 2), (5, 2), (6, 1), (14, 0), (12, 0), (0, 3), (11, 1), (10, 0), (4, 3), (7, 1), (9, 2), (6, 2), (8, 2), (13, 0), (14, 1), (12, 1), (2, 3), (7, 2), (11, 2), (15, 0), (16, 0), (4, 4), (1, 3), (9, 3), (17, 0), (3, 3), (10, 1), (19, 0), (18, 0), (5, 3), (12, 2), (13, 1), (14, 2), (21, 0), (15, 1), (20, 0), (16, 1), (9, 4), (6, 3), (17, 1), (23, 0), (22, 0), (19, 1), (18, 1), (13, 2), (10, 2), (21, 1), (8, 3), (15, 2), (7, 3), (17, 2), (16, 2), (20, 1), (11, 3), (12, 3), (23, 1), (24, 0), (14, 3), (22, 1), (18, 2), (13, 3), (19, 2), (20, 2), (15, 3), (10, 3), (21, 2), (17, 3), (24, 1), (23, 2), (16, 3), (22, 2), (10, 4), (18, 3), (19, 3), (24, 2), (20, 3), (21, 3), (23, 3), (22, 3), (24, 3))
SERVE = (1, 2, 3, 4, 5, 6, 8, 8, 11, 13, 15, 16, 17, 19, 19, 20, 21, 24, 25, 26, 26, 28, 31, 33, 33, 37, 38, 39, 48, 52, 55, 57, 59, 60, 63, 65, 67, 67, 70, 72, 76, 77, 82, 83, 86, 88, 89, 90)


class Plan:
    def __init__(self, tables, seq, width, heads, hidden, dp):
        self.tables, self.seq, self.width, self.heads, self.hidden, self.dp = tables, seq, width, heads, hidden, dp
        self.rows = tables * seq
        self.share = width // dp
        self.fused = dp == 16 and self.share % 16 == 0
        self.step = 256
        steps = hidden // self.step
        chunks = []
        self.z_columns = 0
        self.z_at = []
        for c in range(steps):
            for name, at in (("down", 0), ("up", hidden)):
                chunks.append((name, at + c * self.step, self.step))
        at = 2 * hidden
        self.first = {"down": 0, "up": hidden}
        self.piece = 128
        for name in ("out", "q", "k", "v"):
            self.first[name] = at
            for j in range(heads // self.piece):
                chunks.append((name, at, self.piece))
                at += self.piece
        self.first["vec"] = at
        chunks.append(("vec", at, 128))
        chunks = [c + (HOPS[i % len(HOPS)],) for i, c in enumerate(chunks)]
        for _, _, cw, kind in chunks:
            self.z_at.append(self.z_columns)
            self.z_columns += cw if kind[0] == "z" else 0
        self.chunks = chunks
        self.columns = at + 128
        self.finish_parts = (8, 4, 1, 1, 1, 1)
        if self.fused:
            shapes = ((self.share, hidden), (self.share, hidden), (self.share, heads), (3, self.share, heads), (8, self.share))
            self.grad_shapes = tuple((a, F32) for a in shapes)
        else:
            self.grad_shapes = (((width, self.columns), BF),)


def layer_kernel(
    plan,
    counts_ref, x_hbm, wqkv_hbm, wout_hbm, wup_hbm, wdown_hbm, cot_hbm, g1_ref, b1_ref, g2_ref, b2_ref,
    out_hbm, gin_hbm, *rest,
):
    grads_hbm, rest = rest[: len(plan.grad_shapes)], rest[len(plan.grad_shapes) :]
    (
        x, wqkv, wout, wup, wdown, gl,
    nrm, q, k, v, prob, ho, resid, gres, n2, n2t, glt, act, glf, vec,
    xs, xr_a, xr_b, mr,
    g, r1, r2, r3, r4, red, vecs,
    in_sem, out_sem, red_sem, xsend, xrecv, send, recv,
    ) = rest
    T, S, D, H, FF = plan.tables, plan.seq, plan.width, plan.heads, plan.hidden
    R = plan.rows
    pairs = H // PAIR
    dp = lax.axis_index("dp")
    mp = lax.axis_index("mp")
    xx, yy, zz = lax.rem(dp, 2), lax.rem(lax.div(dp, 2), 2), lax.div(dp, 4)
    partner = (dp, 1 - mp)

    def chip(z, y, x_):
        return (z * 4 + y * 2 + x_, mp)

    x_peer, y_peer = chip(zz, yy, 1 - xx), chip(zz, 1 - yy, xx)
    z_peers = [chip(lax.rem(zz + d, 4), yy, xx) for d in (1, 2, 3)]
    peers = [partner] + ([x_peer, y_peer] + z_peers if plan.fused else [])

    loads = [
        pltpu.make_async_copy(a, b, in_sem.at[i])
        for i, (a, b) in enumerate(
            ((x_hbm, x), (wqkv_hbm, wqkv), (wout_hbm, wout), (cot_hbm, gl), (wup_hbm, wup), (wdown_hbm, wdown))
        )
    ]
    for c in loads:
        c.start()
    barrier = pltpu.get_barrier_semaphore()
    for n in peers:
        pl.semaphore_signal(barrier, inc=1, device_id=n, device_id_type=MESH)
    pl.semaphore_wait(barrier, len(peers))

    def remote(src, dst, ss, rs, dev):
        return pltpu.make_async_remote_copy(src, dst, ss, rs, device_id=dev, device_id_type=MESH)

    def swap(i, t, src, dst):
        rows = pl.ds(t * S, S)
        return remote(src.at[rows], dst.at[rows], xsend.at[i, t], xrecv.at[i, t], partner)

    zh, zl = lax.div(zz, 2), lax.rem(zz, 2)
    outer = lax.rem(zh + zl + 1, 2)

    stores = {}

    def store(i):
        name, c0, cw, _ = plan.chunks[i]
        off = c0 - plan.first[name]
        if name == "vec":
            vecs[...] = red[:, c0 : c0 + cw].T
            stores[i] = pltpu.make_async_copy(vecs.at[0:8], grads_hbm[4], red_sem.at[i])
        else:
            at = {"down": 0, "up": 1, "out": 2, "q": 3, "k": 3, "v": 3}[name]
            dst = grads_hbm[at].at["qkv".index(name)] if at == 3 else grads_hbm[at]
            stores[i] = pltpu.make_async_copy(red.at[:, pl.ds(c0, cw)], dst.at[:, pl.ds(off, cw)], red_sem.at[i])
        stores[i].start()

    def add(dst, a, b):
        dst[...] = (a[...].astype(F32) + b[...].astype(F32)).astype(BF)

    def flat(i):
        _, c0, cw, kind = plan.chunks[i]
        cs = pl.ds(c0, cw)
        isx = kind == "x"
        other, mine = (1 - yy, yy) if isx else (1 - xx, xx)
        c1 = remote(
            g.at[:, :, :, 1 - xx, :, cs] if isx else g.at[:, :, 1 - yy, :, :, cs],
            r1.at[:, :, :, :, cs], send.at[i, 0], recv.at[i, 0], x_peer if isx else y_peer,
        )
        c2 = remote(r1.at[:, :, other, :, cs], r2.at[:, :, :, cs], send.at[i, 1], recv.at[i, 1], y_peer if isx else x_peer)
        c3 = []
        for d in (1, 2, 3):
            z = lax.rem(zz + d, 4)
            c3.append(
                remote(r2.at[lax.div(z, 2), lax.rem(z, 2), :, cs], r3.at[d - 1, :, cs], send.at[i, 1 + d], recv.at[i, 1 + d], z_peers[d - 1])
            )

        def add_one():
            c1.wait_recv()

            def part(p):
                for h in range(2):
                    for l in range(2):
                        own = g.at[h, l, p, xx, :, cs] if isx else g.at[h, l, yy, p, :, cs]
                        add(r1.at[h, l, p, :, cs], own, r1.at[h, l, p, :, cs])

            part(other)
            c2.start()
            part(mine)

        def add_two():
            c2.wait_recv()
            for d in (2, 3, 1, 0):
                z = lax.rem(zz + d, 4)
                h, l = lax.div(z, 2), lax.rem(z, 2)
                add(r2.at[h, l, :, cs], r1.at[h, l, mine, :, cs], r2.at[h, l, :, cs])
                if d:
                    c3[d - 1].start()

        def add_three():
            for c in c3:
                c.wait_recv()
            total = r2[zh, zl, :, cs].astype(F32)
            for d in range(3):
                total = total + r3[d, :, cs].astype(F32)
            red[:, cs] = total
            store(i)

        def drain():
            for c in (c1, c2, *c3):
                c.wait_send()

        return [c1.start, add_one, add_two, add_three], drain

    def upright(i):
        _, c0, cw, kind = plan.chunks[i]
        cs, zs = pl.ds(c0, cw), pl.ds(plan.z_at[i], cw)
        isx = kind == "zx"
        kept = jnp.where(outer == 1, zh, 1 - zh)
        mate = chip(zh * 2 + 1 - zl, yy, xx)
        across_mid = chip(3 - zz, yy, xx)
        across_end = chip((1 - zh) * 3, yy, xx)
        ca = remote(g.at[1 - kept, :, :, :, :, cs], r1.at[:, :, :, :, cs], send.at[i, 0], recv.at[i, 0], mate)
        end_b = remote(r1.at[1 - zl, :, :, :, cs], r4.at[:, :, :, zs], send.at[i, 1], recv.at[i, 1], mate)
        mid_b = remote(r1.at[1 - zl, :, :, :, cs], r2.at[:, :, :, cs], send.at[i, 1], recv.at[i, 2], across_mid)
        far_b = remote(r1.at[zl, :, :, :, cs], r2.at[:, :, :, cs], send.at[i, 2], recv.at[i, 2], across_end)
        if isx:
            half, single = r2.at[:, 1 - xx, :, cs], r2.at[1 - yy, xx, :, cs]
        else:
            half, single = r2.at[1 - yy, :, :, cs], r2.at[yy, 1 - xx, :, cs]
        cc = remote(half, r3.at[0:2, :, cs], send.at[i, 3], recv.at[i, 3], x_peer if isx else y_peer)
        cd = remote(single, r3.at[2, :, cs], send.at[i, 4], recv.at[i, 4], y_peer if isx else x_peer)

        def add_one():
            ca.wait_recv()
            for l in range(2):
                for y in range(2):
                    for x_ in range(2):
                        add(r1.at[l, y, x_, :, cs], g.at[kept, l, y, x_, :, cs], r1.at[l, y, x_, :, cs])

            @pl.when(outer == 1)
            def _():
                end_b.start()

            @pl.when(outer == 0)
            def _():
                mid_b.start()
                far_b.start()

        def add_two():
            mid_b.wait_recv()

            @pl.when(outer == 0)
            def _():
                end_b.wait_recv()

            def part(y, x_):
                @pl.when(outer == 1)
                def _():
                    add(r2.at[y, x_, :, cs], r1.at[zl, y, x_, :, cs], r2.at[y, x_, :, cs])

                @pl.when(outer == 0)
                def _():
                    add(r2.at[y, x_, :, cs], r4.at[y, x_, :, zs], r2.at[y, x_, :, cs])

            for p in range(2):
                part(p, 1 - xx) if isx else part(1 - yy, p)
            cc.start()
            for p in range(2):
                part(p, xx) if isx else part(yy, p)

        def add_three():
            cc.wait_recv()

            def part(p):
                at = r2.at[p, xx, :, cs] if isx else r2.at[yy, p, :, cs]
                add(at, at, r3.at[p, :, cs])

            other, mine = (1 - yy, yy) if isx else (1 - xx, xx)
            part(other)
            cd.start()
            part(mine)

        def add_four():
            cd.wait_recv()
            red[:, cs] = r2[yy, xx, :, cs].astype(F32) + r3[2, :, cs].astype(F32)
            store(i)

        def drain():
            ca.wait_send()

            @pl.when(outer == 1)
            def _():
                end_b.wait_send()

            @pl.when(outer == 0)
            def _():
                mid_b.wait_send()
                far_b.wait_send()

            cc.wait_send()
            cd.wait_send()

        return [ca.start, add_one, add_two, add_three, add_four], drain

    ready = set()
    events = []
    prog = []
    if plan.fused:
        prog = [upright(i) if c[3][0] == "z" else flat(i) for i, c in enumerate(plan.chunks)]
        events = list(ORDER)

    served = [0]

    def service(everything=False):
        limit = len(ORDER) if everything or served[0] >= len(SERVE) else SERVE[served[0]]
        served[0] += 1
        while events and len(ORDER) - len(events) < limit and events[0][0] in ready:
            i, stage = events.pop(0)
            prog[i][0][stage]()

    def made(name, c0, cw):
        for j, c in enumerate(plan.chunks):
            if c0 <= c[1] < c0 + cw:
                ready.add(j)

    def put(c0, cw, rows768):
        cs = pl.ds(c0, cw)
        if plan.fused:
            g[:, :, :, :, :, cs] = rows768.astype(BF).reshape(2, 2, 2, 2, plan.share, cw)
        else:
            g[:, cs] = rows768.astype(BF)

    def blocks(n, body):
        def step(i, carry):
            body(i)
            return carry

        lax.fori_loop(0, n, step, 0)

    def rows_of(b):
        return pl.ds(pl.multiple_of(b * RB, RB), RB)

    loads[0].wait()
    g1, b1, g2, b2 = (a[...].reshape(1, D) for a in (g1_ref, b1_ref, g2_ref, b2_ref))

    def first_norm(b):
        rs = rows_of(b)
        unit, _ = unit_rows(x[rs, :].astype(F32))
        nrm[rs, :] = (unit * g1 + b1).astype(BF)

    blocks(R // RB, first_norm)
    loads[1].wait()

    def project(t):
        all_rows = pl.ds(pl.multiple_of(t * S, S), S)
        context = pl.ds(pl.multiple_of(t * S, S), CTX)
        q[all_rows, :] = nn(nrm[all_rows, :], wqkv[0]).astype(BF)
        kept = pl.ds(pl.multiple_of(t * CTX, CTX), CTX)
        k[kept, :] = nn(nrm[context, :], wqkv[1]).astype(BF)
        v[kept, :] = nn(nrm[context, :], wqkv[2]).astype(BF)

    blocks(T, project)

    scale = 1.0 / math.sqrt(HD)
    low_lane = lax.broadcasted_iota(jnp.int32, (CTX, PAIR), 1) < HD
    low_row = lax.broadcasted_iota(jnp.int32, (PAIR, CTX), 0) < HD

    def stacked(a):
        zero = jnp.zeros_like(a)
        return jnp.concatenate([jnp.where(low_lane, a, zero), jnp.where(low_lane, zero, a)], axis=0)

    def beside(a):
        at = a.T
        zero = jnp.zeros_like(at)
        return jnp.concatenate([jnp.where(low_row, at, zero), jnp.where(low_row, zero, at)], axis=1)

    def merged(a):
        return jnp.where(low_lane, a[:CTX], a[CTX:])

    def attend(t, h):
        rows = pl.ds(pl.multiple_of(t * S, S), S)
        kept = pl.ds(pl.multiple_of(t * CTX, CTX), CTX)
        cols = pl.ds(pl.multiple_of(h * PAIR, PAIR), PAIR)
        slot = t * pairs + h
        scores = nt(stacked(k[kept, cols]), q[rows, cols])
        halves = []
        for i in range(2):
            s = scores[i * CTX : (i + 1) * CTX]
            e = jnp.exp((s - jnp.max(s, axis=0, keepdims=True)) * scale)
            p = e * (1.0 / jnp.sum(e, axis=0, keepdims=True))
            prob[slot, i * CTX : (i + 1) * CTX, :] = p
            halves.append(p.astype(BF))
        out_t = nn(beside(v[kept, cols]), jnp.concatenate(halves, axis=0))
        ho[rows, cols] = out_t.T.astype(BF)

    loads[2].wait()
    for t in range(T):
        blocks(pairs, lambda h, t=t: attend(t, h))
        rows = pl.ds(t * S, S)
        xs[rows, :] = nn(ho[rows, :], wout[...]).astype(BF)
        swap(0, t, xs, xr_a).start()

    loads[3].wait()

    def mask(b):
        rs = rows_of(b)
        pos = lax.broadcasted_iota(jnp.int32, (RB, 1), 0) + lax.rem(b * RB, S)
        live = pos < CTX + counts_ref[lax.div(b * RB, S)]
        kept = jnp.where(live, gl[rs, :].astype(F32), 0.0).astype(BF)
        gl[rs, :] = kept
        glt[:, rs] = kept.T

    blocks(R // RB, mask)

    def second_norm(b):
        rs = rows_of(b)
        r = x[rs, :].astype(F32) + (xs[rs, :].astype(F32) + xr_a[rs, :].astype(F32))
        resid[rs, :] = r
        unit, _ = unit_rows(r)
        low = (unit * g2 + b2).astype(BF)
        n2[rs, :] = low
        n2t[:, rs] = low.T

    per = S // RB
    for t in range(T):
        swap(0, t, xs, xr_a).wait_recv()
        blocks(per, lambda i, t=t: second_norm(t * per + i))
    loads[4].wait()
    loads[5].wait()

    def feed(c0, cw):
        cs = pl.ds(c0, cw)

        def body(b):
            rs = rows_of(b)
            lifted = nn(n2[rs, :], wup[:, cs])
            half = 0.5 + 0.5 * lax.erf(lifted * (1.0 / math.sqrt(2.0)))
            act[rs, cs] = (lifted * half).astype(BF)
            slope = half + lifted * (jnp.exp(-0.5 * lifted * lifted) * (1.0 / math.sqrt(2.0 * math.pi)))
            glf[rs, cs] = (slope * nt(gl[rs, :], wdown[cs, :])).astype(BF)

        blocks(R // RB, body)

    def grad(name, c0, left, right, r0, cw):
        at = plan.first[name] + c0
        put(at, cw, nn(left, right[:, r0 : r0 + cw]))
        made(name, at, cw)

    for c in range(FF // plan.step):
        c0 = c * plan.step
        feed(c0, plan.step)
        grad("down", c0, glt[...], act, c0, plan.step)
        service()
        grad("up", c0, n2t[...], glf, c0, plan.step)
        service()

    for t in range(T):
        swap(0, t, xs, xr_a).wait_send()
    for t in range(T):
        rows = pl.ds(t * S, S)
        for j in range(D // 256):
            xs[rows, j * 256 : (j + 1) * 256] = nt(glf[rows, :], wup[j * 256 : (j + 1) * 256, :]).astype(BF)
            service()
        swap(1, t, xs, xr_b).start()

    vec[...] = jnp.zeros_like(vec)

    def second_back(b):
        rs = rows_of(b)
        grad_norm = xs[rs, :].astype(F32) + xr_b[rs, :].astype(F32)
        unit, inverse = unit_rows(resid[rs, :])
        vec[2:3, :] += jnp.sum(grad_norm * unit, axis=0, keepdims=True)
        vec[3:4, :] += jnp.sum(grad_norm, axis=0, keepdims=True)
        total = gl[rs, :].astype(F32) + norm_backward(grad_norm, unit, inverse, g2)
        gres[rs, :] = total
        low = total.astype(BF)
        gl[rs, :] = low
        n2t[:, rs] = low.T

    for t in range(T):
        swap(1, t, xs, xr_b).wait_recv()
        blocks(per, lambda i, t=t: second_back(t * per + i))
        service()

    gh, gq, gk, gv = 0, H, 2 * H, 3 * H
    for t in range(T):
        rows = slice(t * S, (t + 1) * S)
        glf[rows, gh : gh + H] = nt(gl[rows, :], wout[...]).astype(BF)
    service()
    grad("out", 0, n2t[...], ho, 0, H)
    service()

    def attend_back(t, h):
        rows = pl.ds(pl.multiple_of(t * S, S), S)
        context = pl.ds(pl.multiple_of(t * S, S), CTX)
        kept = pl.ds(pl.multiple_of(t * CTX, CTX), CTX)
        off = pl.multiple_of(h * PAIR, PAIR)
        cols = pl.ds(off, PAIR)
        slot = t * pairs + h
        grad2 = glf[rows, pl.ds(gh + off, PAIR)]
        back = nt(stacked(v[kept, cols]), grad2)
        low_p, low_s = [], []
        for i in range(2):
            p = prob[slot, i * CTX : (i + 1) * CTX, :]
            b = back[i * CTX : (i + 1) * CTX]
            low_p.append(p.astype(BF))
            low_s.append((p * (b - jnp.sum(p * b, axis=0, keepdims=True))).astype(BF))
        low_p = jnp.concatenate(low_p, axis=0)
        low_s = jnp.concatenate(low_s, axis=0)
        glf[rows, pl.ds(gq + off, PAIR)] = (nn(beside(k[kept, cols]), low_s).T * scale).astype(BF)
        glf[context, pl.ds(gk + off, PAIR)] = (merged(nn(low_s, q[rows, cols])) * scale).astype(BF)
        glf[context, pl.ds(gv + off, PAIR)] = merged(nn(low_p, grad2)).astype(BF)

    for t in range(T):
        for h in range(pairs):
            attend_back(t, h)
            service()

    def transpose_normed(b):
        rs = rows_of(b)
        glt[:, rs] = nrm[rs, :].T

    blocks(R // RB, transpose_normed)
    grad("q", 0, glt[...], glf, gq, H)
    service()

    def grad_context(name, r0):
        total = None
        for t in range(T):
            part = nn(glt[:, t * S : t * S + CTX], glf[t * S : t * S + CTX, r0 : r0 + H])
            total = part if total is None else total + part
        put(plan.first[name], H, total)
        made(name, plan.first[name], H)
        service()

    grad_context("k", gk)
    grad_context("v", gv)

    for t in range(T):
        swap(1, t, xs, xr_b).wait_send()
    for t in range(T):
        rows = slice(t * S, (t + 1) * S)
        ctx = slice(t * S, t * S + CTX)
        for j in range(D // 256):
            cs = slice(j * 256, (j + 1) * 256)
            part = nt(glf[rows, gq : gq + H], wqkv[0, cs, :])
            extra = nt(glf[ctx, gk : gk + H], wqkv[1, cs, :]) + nt(glf[ctx, gv : gv + H], wqkv[2, cs, :])
            xs[ctx, cs] = (part[:CTX] + extra).astype(BF)
            xs[t * S + CTX : (t + 1) * S, cs] = part[CTX:].astype(BF)
            service()
        swap(3, t, xs, xr_a).start()

    def feed_out(t):
        rows = slice(t * S, (t + 1) * S)
        for j in range(D // 256):
            cs = slice(j * 256, (j + 1) * 256)
            nrm[rows, cs] = nn(act[rows, :], wdown[:, cs]).astype(BF)
            service()
        swap(2, t, nrm, mr).start()

    feed_out(0)

    def first_back(b):
        rs = rows_of(b)
        grad_norm = xs[rs, :].astype(F32) + xr_a[rs, :].astype(F32)
        unit, inverse = unit_rows(x[rs, :].astype(F32))
        vec[0:1, :] += jnp.sum(grad_norm * unit, axis=0, keepdims=True)
        vec[1:2, :] += jnp.sum(grad_norm, axis=0, keepdims=True)
        gres[rs, :] = gres[rs, :] + norm_backward(grad_norm, unit, inverse, g1)

    for t in range(T):
        swap(3, t, xs, xr_a).wait_recv()
        blocks(per, lambda i, t=t: first_back(t * per + i))
        service()
    store_gin = pltpu.make_async_copy(gres, gin_hbm, out_sem.at[1])
    store_gin.start()
    put(plan.first["vec"], 128, jnp.concatenate([vec[...], jnp.zeros((128 - vec.shape[0], D), F32)], axis=0).T)
    made("vec", plan.first["vec"], 128)
    service()

    for t in range(1, T):
        feed_out(t)

    def output(b):
        rs = rows_of(b)
        pos = lax.broadcasted_iota(jnp.int32, (RB, 1), 0) + lax.rem(b * RB, S)
        live = pos < CTX + counts_ref[lax.div(b * RB, S)]
        total = resid[rs, :] + (nrm[rs, :].astype(F32) + mr[rs, :].astype(F32))
        n2[rs, :] = jnp.where(live, total, 0.0).astype(BF)

    for t in range(T):
        swap(2, t, nrm, mr).wait_recv()
        blocks(per, lambda i, t=t: output(t * per + i))
        service()
    store_out = pltpu.make_async_copy(n2, out_hbm, out_sem.at[0])
    store_out.start()
    service(True)
    assert not events

    if not plan.fused:
        stores[0] = pltpu.make_async_copy(g, grads_hbm[0], red_sem.at[0])
        stores[0].start()
    for p in prog:
        p[1]()
    for t in range(T):
        swap(2, t, nrm, mr).wait_send()
        swap(3, t, xs, xr_a).wait_send()
    store_out.wait()
    store_gin.wait()
    for c in stores.values():
        c.wait()


def run_layer(plan, counts, x, wqkv, wout, wup, wdown, cot, gains):
    R, D, H, FF, W = plan.rows, plan.width, plan.heads, plan.hidden, plan.columns
    V = pltpu.VMEM
    DMA = pltpu.SemaphoreType.DMA
    n = len(plan.chunks)
    share = plan.share
    if plan.fused:
        gshape = (2, 2, 2, 2, share, W)
        comm = [V((2, 2, 2, share, W), BF), V((2, 2, share, W), BF), V((3, share, W), BF)]
        comm += [V((2, 2, share, plan.z_columns), BF), V((share, W), F32), V((128, share), F32)]
    else:
        gshape = (D, W)
        comm = [V((8, 128), F32)] * 6
    scratch = [
        V((R, D), BF), V((3, D, H), BF), V((H, D), BF), V((D, FF), BF), V((FF, D), BF), V((R, D), BF),
        V((R, D), BF), V((R, H), BF), V((plan.tables * CTX, H), BF), V((plan.tables * CTX, H), BF),
        V((plan.tables * (H // PAIR), 2 * CTX, plan.seq), F32), V((R, H), BF), V((R, D), F32), V((R, D), F32), V((R, D), BF),
        V((D, R), BF), V((D, R), BF), V((R, FF), BF), V((R, FF), BF), V((8, D), F32),
        V((R, D), BF), V((R, D), BF), V((R, D), BF), V((R, D), BF),
        V(gshape, BF), *comm,
        DMA((6,)), DMA((2,)), DMA((n,)), DMA((4, plan.tables)), DMA((4, plan.tables)),
        DMA((n, 5)), DMA((n, 5)),
    ]
    hbm = pl.BlockSpec(memory_space=pl.ANY)

    def kernel(*refs):
        layer_kernel(plan, *refs)

    return pl.pallas_call(
        kernel,
        out_shape=(
            jax.ShapeDtypeStruct((R, D), BF),
            jax.ShapeDtypeStruct((R, D), F32),
            *(jax.ShapeDtypeStruct(*a) for a in plan.grad_shapes),
        ),
        in_specs=[pl.BlockSpec(memory_space=pltpu.SMEM)] + [hbm] * 6 + [pl.BlockSpec(memory_space=pltpu.VMEM)] * 4,
        out_specs=(hbm,) * (2 + len(plan.grad_shapes)),
        scratch_shapes=scratch,
        compiler_params=pltpu.CompilerParams(collective_id=0, has_side_effects=True, vmem_limit_bytes=67043328),
        name="layer",
    )(counts, x, wqkv, wout, wup, wdown, cot, *gains)


def finish_kernel(plan, *refs):
    n = 6
    src, vec_ref, dst, vec_out = refs[:n], refs[n], refs[n + 1 : 2 * n + 1], refs[2 * n + 1 : 2 * n + 5]
    bufs, in_sem, out_sem = refs[2 * n + 5 : 3 * n + 5], refs[3 * n + 5], refs[3 * n + 6]
    moves = []
    for i in range(n):
        rows = src[i].shape[0]
        parts = plan.finish_parts[i]
        for j in range(parts):
            moves.append((i, pl.ds(j * (rows // parts), rows // parts)))
    loads, stores = [], []
    for m, (i, rows) in enumerate(moves):
        loads.append(pltpu.make_async_copy(src[i].at[rows], bufs[i].at[rows], in_sem.at[m]))
        stores.append(pltpu.make_async_copy(bufs[i].at[rows], dst[i].at[rows], out_sem.at[m]))
    for c in loads:
        c.start()
    for i in range(4):
        vec_out[i][...] = vec_ref[i, :]
    for a, b in zip(loads, stores):
        a.wait()
        b.start()
    for c in stores:
        c.wait()


def finish(plan, shape, out, gin, down, up, o, qkv, vec):
    arrays = (gin, out, up, down, qkv, o)
    n = sum(plan.finish_parts)
    hbm = pl.BlockSpec(memory_space=pltpu.HBM)
    vmem = pl.BlockSpec(memory_space=pltpu.VMEM)
    share = plan.share

    def kernel(*refs):
        finish_kernel(plan, *refs)

    gin, out, up, down, qkv, o, *norms = pl.pallas_call(
        kernel,
        out_shape=tuple(jax.ShapeDtypeStruct(a.shape, a.dtype) for a in arrays)
        + tuple(jax.ShapeDtypeStruct((share,), F32) for _ in range(4)),
        in_specs=[hbm] * 6 + [vmem],
        out_specs=(hbm,) * 6 + (vmem,) * 4,
        scratch_shapes=[pltpu.VMEM(a.shape, a.dtype) for a in arrays]
        + [pltpu.SemaphoreType.DMA((n,)), pltpu.SemaphoreType.DMA((n,))],
        name="finish",
    )(*arrays, vec)
    return (out.reshape(shape), gin.reshape(shape), jnp.transpose(qkv, (1, 0, 2)), o.T, up, down.T, *norms)


def per_device(dp, inputs, counts, w_qkv, w_out, w_up, w_down, gain_one, shift_one, gain_two, shift_two, cotangent):
    tables, seq, width = inputs.shape
    heads, hidden = w_out.shape[0], w_up.shape[1]
    plan = Plan(tables, seq, width, heads, hidden, dp)
    rows = tables * seq
    gains = (gain_one, shift_one, gain_two, shift_two)
    out, gin, *grads = run_layer(
        plan,
        counts,
        inputs.reshape(rows, width),
        jnp.transpose(w_qkv, (1, 0, 2)),
        w_out,
        w_up,
        w_down,
        cotangent.reshape(rows, width),
        gains,
    )
    if plan.fused:
        down, up, o, qkv, vec = grads
        return finish(plan, inputs.shape, out, gin, down, up, o, qkv, vec)
    else:
        red = lax.psum_scatter(grads[0].astype(F32), "dp", scatter_dimension=0, tiled=True)
        at = 2 * hidden
        down, up, o = red[:, :hidden], red[:, hidden:at], red[:, at : at + heads]
        qkv = red[:, at + heads : at + 4 * heads].reshape(-1, 3, heads).transpose(1, 0, 2)
        vec = red[:, at + 4 * heads : at + 4 * heads + 4].T
    return (
        out.reshape(inputs.shape),
        gin.reshape(inputs.shape),
        jnp.transpose(qkv, (1, 0, 2)),
        o.T,
        up,
        down.T,
        vec[0],
        vec[1],
        vec[2],
        vec[3],
    )


def solution(mesh):
    dp = mesh.shape["dp"]
    in_specs = (
        P("dp", None, None), P("dp"), P(None, None, "mp"), P("mp", None), P(None, "mp"), P("mp", None),
        P(), P(), P(), P(), P("dp", None, None),
    )
    out_specs = (
        P("dp", None, None), P("dp", None, None), P("dp", None, "mp"), P("mp", "dp"), P("dp", "mp"), P("mp", "dp"),
        P("dp"), P("dp"), P("dp"), P("dp"),
    )

    def step(*args):
        return per_device(dp, *args)

    return jax.shard_map(step, mesh=mesh, in_specs=in_specs, out_specs=out_specs, check_vma=False)
```

time: 127 us -> 102 us (0.80)
  local copies, waits for them, and re-layouts: 14.8 us -> 0 us
  Pallas kernels: 110 us -> 101 us
    pallas_call x1, Pallas kernels: 110 us -> 94.6 us  [run_layer(): pl.pallas_call(kernel, out_shape=(jax.ShapeDtypeStruct((R, D), BF), jax.S...]
    pallas_call x0 -> x1, Pallas kernels: none -> 6.28 us  [finish(): pl.pallas_call(kernel, out_shape=tuple((jax.ShapeDtypeStruct(a.shape, a.d...]
    unnamed x15 -> x0, local copies, waits for them, and re-layouts: 5.47 us -> none
    transpose x2 -> x0, local copies, waits for them, and re-layouts: 3.74 us -> none  [the longest x1 1.9 us: per_device(): red[:, :hidden]]
    reshape x2 -> x0, local copies, waits for them, and re-layouts: 2.91 us -> none  [the longest x1 2.21 us: per_device(): w_qkv.reshape(width, 3 * heads)]
    slice x2 -> x0, local copies, waits for them, and re-layouts: 2.64 us -> none  [the longest x1 1.69 us: per_device(): vec[:, 3]]
where the time goes in v2:
time: 102 us
  Pallas kernels  101 us (99%)
    pallas_call x1, Pallas kernels, run_layer(): pl.pallas_call(kernel, out_shape=(jax.ShapeDtypeStruct((R, D), BF), jax.S...  94.6 us
    pallas_call x1, Pallas kernels, finish(): pl.pallas_call(kernel, out_shape=tuple((jax.ShapeDtypeStruct(a.shape, a.d...  6.28 us

profile of v2, /device:TPU:0, one launch (start us, length us, event | category | flops | bytes accessed | tf_op | source)
XLA Modules:
  0.0 101.7 jit_solution(17006431416713456037)
XLA Ops:
  0.6 94.6 %layer.1 = (bf16[1024,768]{1,0:T(8,128)(2,1)}, f32[1024,768]{1,0:T(8,128)}, f32[48,1536]{1,0:T(8,128)}, f32[48,1536]{1,0:T(8,128)}, f32[48,384]{1,0:T(8,128)}, /*index=5*/f32[3,48,384]{2,1,0:T(8,128)}, f32[8,48]{1,0:T(8,128)}) custom-call(s32[2]{0:T(128)} %refs_0_.1, bf16[1024,768]{1,0:T(8,128)(2,1)} %bitcast.9, bf16[3,768,384]{2,1,0:T(8,128)(2,1)} %bitcast.8, ...), custom_call_target="tpu_custom_call" | custom-call | tf_op jit(solution)/shard_map/layer/pallas_call | solution.py:635
  95.2 6.3 %finish.1 = (f32[1024,768]{1,0:T(8,128)}, bf16[1024,768]{1,0:T(8,128)(2,1)}, f32[48,1536]{1,0:T(8,128)}, f32[48,1536]{1,0:T(8,128)}, f32[3,48,384]{2,1,0:T(8,128...) custom-call(f32[1024,768]{1,0:T(8,128)} %get-tuple-element.27.refs_0_, ...), custom_call_target="tpu_custom_call" | custom-call | tf_op jit(solution)/shard_map/finish/pallas_call | solution.py:685

commit v3 on v2

--- a/solution.py
+++ b/solution.py
@@ -15,6 +15,7 @@
 MESH = pl.DeviceIdType.MESH
 PAIR = 2 * HD
 RB = 256
+NB = 128
 
 
 def nn(a, b):
@@ -23,6 +24,10 @@
 
 def nt(a, b):
     return lax.dot_general(a, b, (((1,), (1,)), ((), ())), preferred_element_type=F32)
+
+
+def tn(a, b):
+    return lax.dot_general(a, b, (((0,), (0,)), ((), ())), preferred_element_type=F32)
 
 
 def unit_rows(rows):
@@ -39,9 +44,10 @@
     return inverse * (u - first - unit * second)
 
 
-HOPS = ('x', 'y', 'x', 'y', 'zy', 'x', 'x', 'x', 'y', 'zy', 'zy', 'y', 'x', 'x', 'y', 'y', 'x', 'y', 'y', 'x', 'y', 'x', 'y', 'x', 'x')
-ORDER = ((0, 0), (1, 0), (2, 0), (3, 0), (4, 0), (5, 0), (0, 1), (1, 1), (2, 1), (8, 0), (3, 1), (4, 1), (9, 0), (0, 2), (6, 0), (5, 1), (2, 2), (11, 0), (1, 2), (7, 0), (3, 2), (8, 1), (9, 1), (4, 2), (5, 2), (6, 1), (14, 0), (12, 0), (0, 3), (11, 1), (10, 0), (4, 3), (7, 1), (9, 2), (6, 2), (8, 2), (13, 0), (14, 1), (12, 1), (2, 3), (7, 2), (11, 2), (15, 0), (16, 0), (4, 4), (1, 3), (9, 3), (17, 0), (3, 3), (10, 1), (19, 0), (18, 0), (5, 3), (12, 2), (13, 1), (14, 2), (21, 0), (15, 1), (20, 0), (16, 1), (9, 4), (6, 3), (17, 1), (23, 0), (22, 0), (19, 1), (18, 1), (13, 2), (10, 2), (21, 1), (8, 3), (15, 2), (7, 3), (17, 2), (16, 2), (20, 1), (11, 3), (12, 3), (23, 1), (24, 0), (14, 3), (22, 1), (18, 2), (13, 3), (19, 2), (20, 2), (15, 3), (10, 3), (21, 2), (17, 3), (24, 1), (23, 2), (16, 3), (22, 2), (10, 4), (18, 3), (19, 3), (24, 2), (20, 3), (21, 3), (23, 3), (22, 3), (24, 3))
-SERVE = (1, 2, 3, 4, 5, 6, 8, 8, 11, 13, 15, 16, 17, 19, 19, 20, 21, 24, 25, 26, 26, 28, 31, 33, 33, 37, 38, 39, 48, 52, 55, 57, 59, 60, 63, 65, 67, 67, 70, 72, 76, 77, 82, 83, 86, 88, 89, 90)
+CHUNKS = (('down', 0, 256), ('up', 0, 256), ('down', 256, 256), ('up', 256, 256), ('down', 512, 512), ('up', 512, 512), ('down', 1024, 512), ('up', 1024, 512), ('out', 0, 384), ('q', 0, 384), ('k', 0, 256), ('k', 256, 128), ('v', 0, 128), ('v', 128, 128), ('v', 256, 128), ('vec', 0, 128))
+HOPS = ('x', 'x', 'y', 'y', 'x', 'zx', 'x', 'y', 'y', 'x', 'y', 'x', 'y', 'y', 'y', 'x')
+ORDER = ((0, 0), (2, 0), (1, 0), (3, 0), (0, 1), (5, 0), (4, 0), (2, 1), (1, 1), (7, 0), (0, 2), (3, 1), (1, 2), (5, 1), (4, 1), (6, 0), (0, 3), (2, 2), (3, 2), (8, 0), (7, 1), (4, 2), (1, 3), (5, 2), (6, 1), (9, 0), (2, 3), (3, 3), (7, 2), (8, 1), (10, 0), (5, 3), (6, 2), (12, 0), (4, 3), (9, 1), (10, 1), (11, 0), (13, 0), (5, 4), (7, 3), (8, 2), (14, 0), (12, 1), (6, 3), (10, 2), (9, 2), (11, 1), (15, 0), (12, 2), (13, 1), (8, 3), (14, 1), (11, 2), (15, 1), (10, 3), (13, 2), (14, 2), (9, 3), (15, 2), (12, 3), (11, 3), (13, 3), (14, 3), (15, 3))
+SERVE = (1, 3, 4, 7, 8, 10, 12, 16, 16, 18, 20, 21, 22, 25, 26, 31, 34, 39, 44, 46, 47, 49, 51, 53, 55)
 
 
 class Plan:
@@ -51,23 +57,17 @@
         self.share = width // dp
         self.fused = dp == 16 and self.share % 16 == 0
         self.step = 256
-        steps = hidden // self.step
-        chunks = []
+        self.first = {"down": 0, "up": hidden, "out": 2 * hidden}
+        for name, before in (("q", "out"), ("k", "q"), ("v", "k"), ("vec", "v")):
+            self.first[name] = self.first[before] + heads
+        at = self.first["vec"]
         self.z_columns = 0
         self.z_at = []
-        for c in range(steps):
-            for name, at in (("down", 0), ("up", hidden)):
-                chunks.append((name, at + c * self.step, self.step))
-        at = 2 * hidden
-        self.first = {"down": 0, "up": hidden}
-        self.piece = 128
-        for name in ("out", "q", "k", "v"):
-            self.first[name] = at
-            for j in range(heads // self.piece):
-                chunks.append((name, at, self.piece))
-                at += self.piece
-        self.first["vec"] = at
-        chunks.append(("vec", at, 128))
+        if hidden == 1536 and heads == 384:
+            widths = CHUNKS
+        else:
+            widths = (("down", 0, hidden), ("up", 0, hidden), *((n, 0, heads) for n in ("out", "q", "k", "v")), ("vec", 0, 128))
+        chunks = [(name, self.first[name] + off, cw) for name, off, cw in widths]
         chunks = [c + (HOPS[i % len(HOPS)],) for i, c in enumerate(chunks)]
         for _, _, cw, kind in chunks:
             self.z_at.append(self.z_columns)
@@ -90,8 +90,8 @@
     grads_hbm, rest = rest[: len(plan.grad_shapes)], rest[len(plan.grad_shapes) :]
     (
         x, wqkv, wout, wup, wdown, gl,
-    nrm, q, k, v, prob, ho, resid, gres, n2, n2t, glt, act, glf, vec,
-    xs, xr_a, xr_b, mr,
+    nrm, q, k, v, prob, ho, resid, gres, glt, n2t, act, glf, vec, work, low_s,
+    xs, xr_a, xr_b,
     g, r1, r2, r3, r4, red, vecs,
     in_sem, out_sem, red_sem, xsend, xrecv, send, recv,
     ) = rest
@@ -121,7 +121,6 @@
     barrier = pltpu.get_barrier_semaphore()
     for n in peers:
         pl.semaphore_signal(barrier, inc=1, device_id=n, device_id_type=MESH)
-    pl.semaphore_wait(barrier, len(peers))
 
     def remote(src, dst, ss, rs, dev):
         return pltpu.make_async_remote_copy(src, dst, ss, rs, device_id=dev, device_id_type=MESH)
@@ -132,20 +131,23 @@
 
     zh, zl = lax.div(zz, 2), lax.rem(zz, 2)
     outer = lax.rem(zh + zl + 1, 2)
-
-    stores = {}
 
     def store(i):
         name, c0, cw, _ = plan.chunks[i]
         off = c0 - plan.first[name]
         if name == "vec":
-            vecs[...] = red[:, c0 : c0 + cw].T
-            stores[i] = pltpu.make_async_copy(vecs.at[0:8], grads_hbm[4], red_sem.at[i])
+            return pltpu.make_async_copy(vecs.at[0:8], grads_hbm[4], red_sem.at[i])
+        at = {"down": 0, "up": 1, "out": 2, "q": 3, "k": 3, "v": 3}[name]
+        dst = grads_hbm[at].at["qkv".index(name)] if at == 3 else grads_hbm[at]
+        return pltpu.make_async_copy(red.at[:, pl.ds(c0, cw)], dst.at[:, pl.ds(off, cw)], red_sem.at[i])
+
+    def finished(i, total):
+        name, c0, cw, _ = plan.chunks[i]
+        if name == "vec":
+            vecs[...] = total.T
         else:
-            at = {"down": 0, "up": 1, "out": 2, "q": 3, "k": 3, "v": 3}[name]
-            dst = grads_hbm[at].at["qkv".index(name)] if at == 3 else grads_hbm[at]
-            stores[i] = pltpu.make_async_copy(red.at[:, pl.ds(c0, cw)], dst.at[:, pl.ds(off, cw)], red_sem.at[i])
-        stores[i].start()
+            red[:, pl.ds(c0, cw)] = total
+        store(i).start()
 
     def add(dst, a, b):
         dst[...] = (a[...].astype(F32) + b[...].astype(F32)).astype(BF)
@@ -171,10 +173,12 @@
             c1.wait_recv()
 
             def part(p):
-                for h in range(2):
-                    for l in range(2):
-                        own = g.at[h, l, p, xx, :, cs] if isx else g.at[h, l, yy, p, :, cs]
-                        add(r1.at[h, l, p, :, cs], own, r1.at[h, l, p, :, cs])
+                def one(j):
+                    h, l = lax.div(j, 2), lax.rem(j, 2)
+                    own = g.at[h, l, p, xx, :, cs] if isx else g.at[h, l, yy, p, :, cs]
+                    add(r1.at[h, l, p, :, cs], own, r1.at[h, l, p, :, cs])
+
+                loop(4, one)
 
             part(other)
             c2.start()
@@ -195,8 +199,7 @@
             total = r2[zh, zl, :, cs].astype(F32)
             for d in range(3):
                 total = total + r3[d, :, cs].astype(F32)
-            red[:, cs] = total
-            store(i)
+            finished(i, total)
 
         def drain():
             for c in (c1, c2, *c3):
@@ -225,10 +228,12 @@
 
         def add_one():
             ca.wait_recv()
-            for l in range(2):
-                for y in range(2):
-                    for x_ in range(2):
-                        add(r1.at[l, y, x_, :, cs], g.at[kept, l, y, x_, :, cs], r1.at[l, y, x_, :, cs])
+
+            def one(j):
+                l, y, x_ = lax.div(j, 4), lax.rem(lax.div(j, 2), 2), lax.rem(j, 2)
+                add(r1.at[l, y, x_, :, cs], g.at[kept, l, y, x_, :, cs], r1.at[l, y, x_, :, cs])
+
+            loop(8, one)
 
             @pl.when(outer == 1)
             def _():
@@ -275,8 +280,7 @@
 
         def add_four():
             cd.wait_recv()
-            red[:, cs] = r2[yy, xx, :, cs].astype(F32) + r3[2, :, cs].astype(F32)
-            store(i)
+            finished(i, r2[yy, xx, :, cs].astype(F32) + r3[2, :, cs].astype(F32))
 
         def drain():
             ca.wait_send()
@@ -295,26 +299,27 @@
 
         return [ca.start, add_one, add_two, add_three, add_four], drain
 
-    ready = set()
-    events = []
     prog = []
     if plan.fused:
         prog = [upright(i) if c[3][0] == "z" else flat(i) for i, c in enumerate(plan.chunks)]
-        events = list(ORDER)
-
-    served = [0]
-
-    def service(everything=False):
-        limit = len(ORDER) if everything or served[0] >= len(SERVE) else SERVE[served[0]]
-        served[0] += 1
-        while events and len(ORDER) - len(events) < limit and events[0][0] in ready:
-            i, stage = events.pop(0)
-            prog[i][0][stage]()
-
-    def made(name, c0, cw):
-        for j, c in enumerate(plan.chunks):
-            if c0 <= c[1] < c0 + cw:
-                ready.add(j)
+
+    def due(first, last=None):
+        if plan.fused:
+            start = SERVE[first - 1] if first else 0
+            for i, stage in ORDER[start : SERVE[first] if last is None else len(ORDER)]:
+                prog[i][0][stage]()
+
+    def due_in(j, n, first, stride=1):
+        for i in range(n):
+            if plan.fused and SERVE[first + i * stride] > (SERVE[first + i * stride - 1] if first + i * stride else 0):
+                pl.when(j == i)(lambda i=i: due(first + i * stride))
+
+    def loop(n, body):
+        def step(i, carry):
+            body(i)
+            return carry
+
+        lax.fori_loop(0, n, step, 0)
 
     def put(c0, cw, rows768):
         cs = pl.ds(c0, cw)
@@ -323,13 +328,6 @@
         else:
             g[:, cs] = rows768.astype(BF)
 
-    def blocks(n, body):
-        def step(i, carry):
-            body(i)
-            return carry
-
-        lax.fori_loop(0, n, step, 0)
-
     def rows_of(b):
         return pl.ds(pl.multiple_of(b * RB, RB), RB)
 
@@ -341,18 +339,19 @@
         unit, _ = unit_rows(x[rs, :].astype(F32))
         nrm[rs, :] = (unit * g1 + b1).astype(BF)
 
-    blocks(R // RB, first_norm)
-    loads[1].wait()
-
-    def project(t):
-        all_rows = pl.ds(pl.multiple_of(t * S, S), S)
-        context = pl.ds(pl.multiple_of(t * S, S), CTX)
-        q[all_rows, :] = nn(nrm[all_rows, :], wqkv[0]).astype(BF)
-        kept = pl.ds(pl.multiple_of(t * CTX, CTX), CTX)
+    per = S // RB
+    for t in range(T):
+        for i in range(per):
+            first_norm(t * per + i)
+        if t == 0:
+            loads[1].wait()
+        rows, context, kept = slice(t * S, (t + 1) * S), slice(t * S, t * S + CTX), slice(t * CTX, (t + 1) * CTX)
+        q[rows, :] = nn(nrm[rows, :], wqkv[0]).astype(BF)
         k[kept, :] = nn(nrm[context, :], wqkv[1]).astype(BF)
         v[kept, :] = nn(nrm[context, :], wqkv[2]).astype(BF)
 
-    blocks(T, project)
+    n2 = x
+    low_p = n2.at[0 : 2 * CTX, 0:S]
 
     scale = 1.0 / math.sqrt(HD)
     low_lane = lax.broadcasted_iota(jnp.int32, (CTX, PAIR), 1) < HD
@@ -370,28 +369,35 @@
     def merged(a):
         return jnp.where(low_lane, a[:CTX], a[CTX:])
 
+    def attend_scores(t, h):
+        rows, kept, cols = slice(t * S, (t + 1) * S), slice(t * CTX, (t + 1) * CTX), slice(h * PAIR, (h + 1) * PAIR)
+        prob[t * pairs + h] = nt(stacked(k[kept, cols]), q[rows, cols])
+
     def attend(t, h):
-        rows = pl.ds(pl.multiple_of(t * S, S), S)
-        kept = pl.ds(pl.multiple_of(t * CTX, CTX), CTX)
-        cols = pl.ds(pl.multiple_of(h * PAIR, PAIR), PAIR)
+        rows, kept, cols = slice(t * S, (t + 1) * S), slice(t * CTX, (t + 1) * CTX), slice(h * PAIR, (h + 1) * PAIR)
         slot = t * pairs + h
-        scores = nt(stacked(k[kept, cols]), q[rows, cols])
-        halves = []
         for i in range(2):
-            s = scores[i * CTX : (i + 1) * CTX]
+            part = slice(i * CTX, (i + 1) * CTX)
+            s = prob[slot, part, :]
             e = jnp.exp((s - jnp.max(s, axis=0, keepdims=True)) * scale)
             p = e * (1.0 / jnp.sum(e, axis=0, keepdims=True))
-            prob[slot, i * CTX : (i + 1) * CTX, :] = p
-            halves.append(p.astype(BF))
-        out_t = nn(beside(v[kept, cols]), jnp.concatenate(halves, axis=0))
-        ho[rows, cols] = out_t.T.astype(BF)
-
-    loads[2].wait()
-    for t in range(T):
-        blocks(pairs, lambda h, t=t: attend(t, h))
-        rows = pl.ds(t * S, S)
-        xs[rows, :] = nn(ho[rows, :], wout[...]).astype(BF)
-        swap(0, t, xs, xr_a).start()
+            prob[slot, part, :] = p
+            low_s[part, :] = p.astype(BF)
+        ho[rows, cols] = nn(beside(v[kept, cols]), low_s[...]).T.astype(BF)
+
+    order = [(t, h) for t in range(T) for h in range(pairs)]
+    attend_scores(*order[0])
+    for j, (t, h) in enumerate(order):
+        if j + 1 < len(order):
+            attend_scores(*order[j + 1])
+        attend(t, h)
+        if h == pairs - 1:
+            if t == 0:
+                loads[2].wait()
+                pl.semaphore_wait(barrier, len(peers))
+            rows = slice(t * S, (t + 1) * S)
+            xs[rows, :] = nn(ho[rows, :], wout[...]).astype(BF)
+            swap(0, t, xs, xr_a).start()
 
     loads[3].wait()
 
@@ -403,205 +409,250 @@
         gl[rs, :] = kept
         glt[:, rs] = kept.T
 
-    blocks(R // RB, mask)
+    loop(R // RB, mask)
 
     def second_norm(b):
         rs = rows_of(b)
         r = x[rs, :].astype(F32) + (xs[rs, :].astype(F32) + xr_a[rs, :].astype(F32))
         resid[rs, :] = r
         unit, _ = unit_rows(r)
-        low = (unit * g2 + b2).astype(BF)
-        n2[rs, :] = low
-        n2t[:, rs] = low.T
-
-    per = S // RB
+        n2[rs, :] = (unit * g2 + b2).astype(BF)
+
     for t in range(T):
         swap(0, t, xs, xr_a).wait_recv()
-        blocks(per, lambda i, t=t: second_norm(t * per + i))
+        loop(per, lambda i, t=t: second_norm(t * per + i))
     loads[4].wait()
     loads[5].wait()
 
-    def feed(c0, cw):
-        cs = pl.ds(c0, cw)
-
-        def body(b):
-            rs = rows_of(b)
-            lifted = nn(n2[rs, :], wup[:, cs])
+    step = plan.step
+    steps = FF // step
+
+    def hidden_of(c):
+        return pl.ds(c * step if isinstance(c, int) else pl.multiple_of(c * step, step), step)
+
+    def lift(c):
+        work[0] = nn(n2[...], wup[:, hidden_of(c)])
+
+    def pull(c):
+        work[1] = nt(gl[...], wdown[hidden_of(c), :])
+
+    def bend(c):
+        cs = hidden_of(c)
+        for b in range(R // RB):
+            rs = slice(b * RB, (b + 1) * RB)
+            lifted = work[0, rs, :]
             half = 0.5 + 0.5 * lax.erf(lifted * (1.0 / math.sqrt(2.0)))
             act[rs, cs] = (lifted * half).astype(BF)
-            slope = half + lifted * (jnp.exp(-0.5 * lifted * lifted) * (1.0 / math.sqrt(2.0 * math.pi)))
-            glf[rs, cs] = (slope * nt(gl[rs, :], wdown[cs, :])).astype(BF)
-
-        blocks(R // RB, body)
-
-    def grad(name, c0, left, right, r0, cw):
-        at = plan.first[name] + c0
-        put(at, cw, nn(left, right[:, r0 : r0 + cw]))
-        made(name, at, cw)
-
-    for c in range(FF // plan.step):
-        c0 = c * plan.step
-        feed(c0, plan.step)
-        grad("down", c0, glt[...], act, c0, plan.step)
-        service()
-        grad("up", c0, n2t[...], glf, c0, plan.step)
-        service()
+            work[2, rs, :] = half + lifted * (jnp.exp(-0.5 * lifted * lifted) * (1.0 / math.sqrt(2.0 * math.pi)))
+
+    def slope(c):
+        cs = hidden_of(c)
+        for b in range(R // RB):
+            rs = slice(b * RB, (b + 1) * RB)
+            glf[rs, cs] = (work[2, rs, :] * work[1, rs, :]).astype(BF)
+
+    def grad(c0, left_t, right, cols, cw):
+        put(c0, cw, nn(left_t[...], right[:, cols]))
+
+    def feed(c):
+        off = pl.multiple_of(c * step, step)
+        lift(c)
+        pull(c)
+        bend(c)
+        grad(plan.first["down"] + off, glt, act, hidden_of(c), step)
+        slope(c)
+        grad(plan.first["up"] + off, n2t, glf, hidden_of(c), step)
+        due_in(c, steps, 0)
+
+    for b in range(R // RB):
+        n2t[:, b * RB : (b + 1) * RB] = n2[b * RB : (b + 1) * RB, :].T
+    loop(steps, feed)
+    point = steps
 
     for t in range(T):
         swap(0, t, xs, xr_a).wait_send()
-    for t in range(T):
-        rows = pl.ds(t * S, S)
-        for j in range(D // 256):
-            xs[rows, j * 256 : (j + 1) * 256] = nt(glf[rows, :], wup[j * 256 : (j + 1) * 256, :]).astype(BF)
-            service()
+    tiles = D // 256
+    for t in range(T):
+        rows = slice(t * S, (t + 1) * S)
+
+        def body(j, rows=rows):
+            cs = pl.ds(pl.multiple_of(j * 256, 256), 256)
+            xs[rows, cs] = nt(glf[rows, :], wup[cs, :]).astype(BF)
+
+        loop(tiles, body)
         swap(1, t, xs, xr_b).start()
+        due(point)
+        point += 1
 
     vec[...] = jnp.zeros_like(vec)
 
     def second_back(b):
-        rs = rows_of(b)
+        rs = pl.ds(pl.multiple_of(b * NB, NB), NB)
         grad_norm = xs[rs, :].astype(F32) + xr_b[rs, :].astype(F32)
         unit, inverse = unit_rows(resid[rs, :])
         vec[2:3, :] += jnp.sum(grad_norm * unit, axis=0, keepdims=True)
         vec[3:4, :] += jnp.sum(grad_norm, axis=0, keepdims=True)
         total = gl[rs, :].astype(F32) + norm_backward(grad_norm, unit, inverse, g2)
         gres[rs, :] = total
-        low = total.astype(BF)
-        gl[rs, :] = low
-        n2t[:, rs] = low.T
+        gl[rs, :] = total.astype(BF)
 
     for t in range(T):
         swap(1, t, xs, xr_b).wait_recv()
-        blocks(per, lambda i, t=t: second_back(t * per + i))
-        service()
+        loop(S // NB, lambda i, t=t: second_back(t * (S // NB) + i))
+        due(point)
+        point += 1
 
     gh, gq, gk, gv = 0, H, 2 * H, 3 * H
     for t in range(T):
         rows = slice(t * S, (t + 1) * S)
         glf[rows, gh : gh + H] = nt(gl[rows, :], wout[...]).astype(BF)
-    service()
-    grad("out", 0, n2t[...], ho, 0, H)
-    service()
-
-    def attend_back(t, h):
-        rows = pl.ds(pl.multiple_of(t * S, S), S)
-        context = pl.ds(pl.multiple_of(t * S, S), CTX)
-        kept = pl.ds(pl.multiple_of(t * CTX, CTX), CTX)
-        off = pl.multiple_of(h * PAIR, PAIR)
-        cols = pl.ds(off, PAIR)
-        slot = t * pairs + h
-        grad2 = glf[rows, pl.ds(gh + off, PAIR)]
-        back = nt(stacked(v[kept, cols]), grad2)
-        low_p, low_s = [], []
+    put(plan.first["out"], H, tn(gl[...], ho[...]))
+    again = pltpu.make_async_copy(x_hbm, gl, in_sem.at[6])
+    again.start()
+    due(point)
+    point += 1
+
+    half = S // 2
+
+    def back_scores(j, i):
+        t, h = order[j]
+        rows, kept, cols = slice(t * S, (t + 1) * S), slice(t * CTX, (t + 1) * CTX), slice(h * PAIR, (h + 1) * PAIR)
+        part = slice(t * S + i * half, t * S + (i + 1) * half)
+        work[(2 * j + i) % 3, 0 : 2 * CTX, :] = nt(stacked(v[kept, cols]), glf[part, gh + h * PAIR : gh + (h + 1) * PAIR])
+
+    def attend_back(j):
+        t, h = order[j]
+        rows, context = slice(t * S, (t + 1) * S), slice(t * S, t * S + CTX)
+        kept, cols = slice(t * CTX, (t + 1) * CTX), slice(h * PAIR, (h + 1) * PAIR)
         for i in range(2):
-            p = prob[slot, i * CTX : (i + 1) * CTX, :]
-            b = back[i * CTX : (i + 1) * CTX]
-            low_p.append(p.astype(BF))
-            low_s.append((p * (b - jnp.sum(p * b, axis=0, keepdims=True))).astype(BF))
-        low_p = jnp.concatenate(low_p, axis=0)
-        low_s = jnp.concatenate(low_s, axis=0)
-        glf[rows, pl.ds(gq + off, PAIR)] = (nn(beside(k[kept, cols]), low_s).T * scale).astype(BF)
-        glf[context, pl.ds(gk + off, PAIR)] = (merged(nn(low_s, q[rows, cols])) * scale).astype(BF)
-        glf[context, pl.ds(gv + off, PAIR)] = merged(nn(low_p, grad2)).astype(BF)
-
-    for t in range(T):
-        for h in range(pairs):
-            attend_back(t, h)
-            service()
-
-    def transpose_normed(b):
-        rs = rows_of(b)
-        glt[:, rs] = nrm[rs, :].T
-
-    blocks(R // RB, transpose_normed)
-    grad("q", 0, glt[...], glf, gq, H)
-    service()
+            if j + 1 < len(order):
+                back_scores(j + 1, i)
+            side = slice(i * half, (i + 1) * half)
+            for n in range(2):
+                part = slice(n * CTX, (n + 1) * CTX)
+                p = prob[j, part, side]
+                b = work[(2 * j + i) % 3, part, :]
+                low_p[part, side] = p.astype(BF)
+                low_s[part, side] = (p * (b - jnp.sum(p * b, axis=0, keepdims=True))).astype(BF)
+
+        def at(first):
+            return slice(first + h * PAIR, first + (h + 1) * PAIR)
+
+        glf[rows, at(gq)] = (nn(beside(k[kept, cols]), low_s[...]).T * scale).astype(BF)
+        glf[context, at(gk)] = (merged(nn(low_s[...], q[rows, cols])) * scale).astype(BF)
+        glf[context, at(gv)] = merged(nn(low_p[...], glf[rows, at(gh)])).astype(BF)
+
+    back_scores(0, 0)
+    back_scores(0, 1)
+    for j in range(len(order)):
+        attend_back(j)
+        if j % 2 == 1:
+            due(point)
+            point += 1
+
+    for b in range(R // RB):
+        n2t[:, b * RB : (b + 1) * RB] = nrm[b * RB : (b + 1) * RB, :].T
+    grad(plan.first["q"], n2t, glf, slice(gq, gq + H), H)
+    due(point)
 
     def grad_context(name, r0):
         total = None
         for t in range(T):
-            part = nn(glt[:, t * S : t * S + CTX], glf[t * S : t * S + CTX, r0 : r0 + H])
+            part = nn(n2t[:, t * S : t * S + CTX], glf[t * S : t * S + CTX, r0 : r0 + H])
             total = part if total is None else total + part
         put(plan.first[name], H, total)
-        made(name, plan.first[name], H)
-        service()
 
     grad_context("k", gk)
     grad_context("v", gv)
+    due(point + 1)
+    point += 2
 
     for t in range(T):
         swap(1, t, xs, xr_b).wait_send()
     for t in range(T):
         rows = slice(t * S, (t + 1) * S)
         ctx = slice(t * S, t * S + CTX)
-        for j in range(D // 256):
-            cs = slice(j * 256, (j + 1) * 256)
+
+        def body(j, t=t, rows=rows, ctx=ctx):
+            cs = pl.ds(pl.multiple_of(j * 256, 256), 256)
             part = nt(glf[rows, gq : gq + H], wqkv[0, cs, :])
             extra = nt(glf[ctx, gk : gk + H], wqkv[1, cs, :]) + nt(glf[ctx, gv : gv + H], wqkv[2, cs, :])
             xs[ctx, cs] = (part[:CTX] + extra).astype(BF)
             xs[t * S + CTX : (t + 1) * S, cs] = part[CTX:].astype(BF)
-            service()
+
+        loop(tiles, body)
         swap(3, t, xs, xr_a).start()
-
-    def feed_out(t):
+        due(point)
+        point += 1
+
+    def feed_out(t, point):
         rows = slice(t * S, (t + 1) * S)
-        for j in range(D // 256):
-            cs = slice(j * 256, (j + 1) * 256)
+
+        def body(j):
+            cs = pl.ds(pl.multiple_of(j * 256, 256), 256)
             nrm[rows, cs] = nn(act[rows, :], wdown[:, cs]).astype(BF)
-            service()
-        swap(2, t, nrm, mr).start()
-
-    feed_out(0)
+
+        loop(tiles, body)
+        due(point)
+
+    feed_out(0, point)
+    point += 1
 
     def first_back(b):
-        rs = rows_of(b)
+        rs = pl.ds(pl.multiple_of(b * NB, NB), NB)
         grad_norm = xs[rs, :].astype(F32) + xr_a[rs, :].astype(F32)
-        unit, inverse = unit_rows(x[rs, :].astype(F32))
+        unit, inverse = unit_rows(gl[rs, :].astype(F32))
         vec[0:1, :] += jnp.sum(grad_norm * unit, axis=0, keepdims=True)
         vec[1:2, :] += jnp.sum(grad_norm, axis=0, keepdims=True)
         gres[rs, :] = gres[rs, :] + norm_backward(grad_norm, unit, inverse, g1)
 
+    again.wait()
     for t in range(T):
         swap(3, t, xs, xr_a).wait_recv()
-        blocks(per, lambda i, t=t: first_back(t * per + i))
-        service()
+        loop(S // NB, lambda i, t=t: first_back(t * (S // NB) + i))
+        due(point)
+        point += 1
+    swap(2, 0, nrm, xr_b).start()
     store_gin = pltpu.make_async_copy(gres, gin_hbm, out_sem.at[1])
     store_gin.start()
     put(plan.first["vec"], 128, jnp.concatenate([vec[...], jnp.zeros((128 - vec.shape[0], D), F32)], axis=0).T)
-    made("vec", plan.first["vec"], 128)
-    service()
+    due(point)
+    point += 1
 
     for t in range(1, T):
-        feed_out(t)
+        feed_out(t, point)
+        point += 1
+        swap(2, t, nrm, xr_b).start()
 
     def output(b):
         rs = rows_of(b)
         pos = lax.broadcasted_iota(jnp.int32, (RB, 1), 0) + lax.rem(b * RB, S)
         live = pos < CTX + counts_ref[lax.div(b * RB, S)]
-        total = resid[rs, :] + (nrm[rs, :].astype(F32) + mr[rs, :].astype(F32))
+        total = resid[rs, :] + (nrm[rs, :].astype(F32) + xr_b[rs, :].astype(F32))
         n2[rs, :] = jnp.where(live, total, 0.0).astype(BF)
 
     for t in range(T):
-        swap(2, t, nrm, mr).wait_recv()
-        blocks(per, lambda i, t=t: output(t * per + i))
-        service()
+        swap(2, t, nrm, xr_b).wait_recv()
+        loop(per, lambda i, t=t: output(t * per + i))
+        due(point)
+        point += 1
     store_out = pltpu.make_async_copy(n2, out_hbm, out_sem.at[0])
     store_out.start()
-    service(True)
-    assert not events
+    assert point == len(SERVE)
+    due(point, True)
 
     if not plan.fused:
-        stores[0] = pltpu.make_async_copy(g, grads_hbm[0], red_sem.at[0])
-        stores[0].start()
+        store = lambda i: pltpu.make_async_copy(g, grads_hbm[0], red_sem.at[0])
+        store(0).start()
     for p in prog:
         p[1]()
     for t in range(T):
-        swap(2, t, nrm, mr).wait_send()
+        swap(2, t, nrm, xr_b).wait_send()
         swap(3, t, xs, xr_a).wait_send()
     store_out.wait()
     store_gin.wait()
-    for c in stores.values():
-        c.wait()
+    for i in range(max(1, len(prog))):
+        store(i).wait()
 
 
 def run_layer(plan, counts, x, wqkv, wout, wup, wdown, cot, gains):
@@ -620,11 +671,11 @@
     scratch = [
         V((R, D), BF), V((3, D, H), BF), V((H, D), BF), V((D, FF), BF), V((FF, D), BF), V((R, D), BF),
         V((R, D), BF), V((R, H), BF), V((plan.tables * CTX, H), BF), V((plan.tables * CTX, H), BF),
-        V((plan.tables * (H // PAIR), 2 * CTX, plan.seq), F32), V((R, H), BF), V((R, D), F32), V((R, D), F32), V((R, D), BF),
-        V((D, R), BF), V((D, R), BF), V((R, FF), BF), V((R, FF), BF), V((8, D), F32),
-        V((R, D), BF), V((R, D), BF), V((R, D), BF), V((R, D), BF),
+        V((plan.tables * (H // PAIR), 2 * CTX, plan.seq), F32), V((R, H), BF), V((R, D), F32), V((R, D), F32),
+        V((D, R), BF), V((D, R), BF), V((R, FF), BF), V((R, FF), BF), V((8, D), F32), V((3, R, 256), F32), V((2 * CTX, plan.seq), BF),
+        V((R, D), BF), V((R, D), BF), V((R, D), BF),
         V(gshape, BF), *comm,
-        DMA((6,)), DMA((2,)), DMA((n,)), DMA((4, plan.tables)), DMA((4, plan.tables)),
+        DMA((7,)), DMA((2,)), DMA((n,)), DMA((4, plan.tables)), DMA((4, plan.tables)),
         DMA((n, 5)), DMA((n, 5)),
     ]
     hbm = pl.BlockSpec(memory_space=pl.ANY)

time: 102 us -> 93.8 us (0.920)
  Pallas kernels: 101 us -> 92.7 us
    pallas_call x1, Pallas kernels: 94.6 us -> 86.4 us  [run_layer(): pl.pallas_call(kernel, out_shape=(jax.ShapeDtypeStruct((R, D), BF), jax.S...]
where the time goes in v3:
time: 93.8 us; the launch traced here: 93.5 us
  Pallas kernels  92.7 us (99%)
    pallas_call x1, Pallas kernels, run_layer(): pl.pallas_call(kernel, out_shape=(jax.ShapeDtypeStruct((R, D), BF), jax.S...  86.4 us
    pallas_call x1, Pallas kernels, finish(): pl.pallas_call(kernel, out_shape=tuple((jax.ShapeDtypeStruct(a.shape, a.d...  6.28 us

profile of v3, /device:TPU:0, one launch (start us, length us, event | category | flops | bytes accessed | tf_op | source)
XLA Modules:
  0.0 93.5 jit_solution(9344527661669256772)
XLA Ops:
  0.6 86.4 %layer.1 = (bf16[1024,768]{1,0:T(8,128)(2,1)}, f32[1024,768]{1,0:T(8,128)}, f32[48,1536]{1,0:T(8,128)}, f32[48,1536]{1,0:T(8,128)}, f32[48,384]{1,0:T(8,128)}, /*index=5*/f32[3,48,384]{2,1,0:T(8,128)}, f32[8,48]{1,0:T(8,128)}) custom-call(s32[2]{0:T(128)} %refs_0_.1, bf16[1024,768]{1,0:T(8,128)(2,1)} %bitcast.9, bf16[3,768,384]{2,1,0:T(8,128)(2,1)} %bitcast.8, ...), custom_call_target="tpu_custom_call" | custom-call | tf_op jit(solution)/shard_map/layer/pallas_call | solution.py:686
  87.1 6.3 %finish.1 = (f32[1024,768]{1,0:T(8,128)}, bf16[1024,768]{1,0:T(8,128)(2,1)}, f32[48,1536]{1,0:T(8,128)}, f32[48,1536]{1,0:T(8,128)}, f32[3,48,384]{2,1,0:T(8,128...) custom-call(f32[1024,768]{1,0:T(8,128)} %get-tuple-element.27.refs_0_, ...), custom_call_target="tpu_custom_call" | custom-call | tf_op jit(solution)/shard_map/finish/pallas_call | solution.py:736

commit v4 on v3

--- a/solution.py
+++ b/solution.py
@@ -44,10 +44,10 @@
     return inverse * (u - first - unit * second)
 
 
-CHUNKS = (('down', 0, 256), ('up', 0, 256), ('down', 256, 256), ('up', 256, 256), ('down', 512, 512), ('up', 512, 512), ('down', 1024, 512), ('up', 1024, 512), ('out', 0, 384), ('q', 0, 384), ('k', 0, 256), ('k', 256, 128), ('v', 0, 128), ('v', 128, 128), ('v', 256, 128), ('vec', 0, 128))
-HOPS = ('x', 'x', 'y', 'y', 'x', 'zx', 'x', 'y', 'y', 'x', 'y', 'x', 'y', 'y', 'y', 'x')
-ORDER = ((0, 0), (2, 0), (1, 0), (3, 0), (0, 1), (5, 0), (4, 0), (2, 1), (1, 1), (7, 0), (0, 2), (3, 1), (1, 2), (5, 1), (4, 1), (6, 0), (0, 3), (2, 2), (3, 2), (8, 0), (7, 1), (4, 2), (1, 3), (5, 2), (6, 1), (9, 0), (2, 3), (3, 3), (7, 2), (8, 1), (10, 0), (5, 3), (6, 2), (12, 0), (4, 3), (9, 1), (10, 1), (11, 0), (13, 0), (5, 4), (7, 3), (8, 2), (14, 0), (12, 1), (6, 3), (10, 2), (9, 2), (11, 1), (15, 0), (12, 2), (13, 1), (8, 3), (14, 1), (11, 2), (15, 1), (10, 3), (13, 2), (14, 2), (9, 3), (15, 2), (12, 3), (11, 3), (13, 3), (14, 3), (15, 3))
-SERVE = (1, 3, 4, 7, 8, 10, 12, 16, 16, 18, 20, 21, 22, 25, 26, 31, 34, 39, 44, 46, 47, 49, 51, 53, 55)
+CHUNKS = (('down', 0, 256), ('up', 0, 256), ('down', 256, 256), ('up', 256, 256), ('down', 512, 512), ('up', 512, 512), ('down', 1024, 512), ('up', 1024, 512), ('out', 0, 384), ('q', 0, 128), ('q', 128, 256), ('k', 0, 256), ('k', 256, 128), ('v', 0, 128), ('v', 128, 128), ('v', 256, 128))
+HOPS = ('y', 'x', 'y', 'zy', 'x', 'zx', 'x', 'y', 'y', 'zx', 'x', 'x', 'y', 'y', 'y', 'y')
+ORDER = ((0, 0), (1, 0), (3, 0), (2, 0), (0, 1), (1, 1), (5, 0), (4, 0), (3, 1), (0, 2), (1, 2), (2, 1), (7, 0), (5, 1), (6, 0), (3, 2), (4, 1), (2, 2), (7, 1), (8, 0), (3, 3), (4, 2), (5, 2), (0, 3), (1, 3), (6, 1), (2, 3), (7, 2), (10, 0), (3, 4), (8, 1), (12, 0), (9, 0), (5, 3), (13, 0), (4, 3), (6, 2), (11, 0), (14, 0), (10, 1), (12, 1), (5, 4), (7, 3), (9, 1), (8, 2), (13, 1), (15, 0), (6, 3), (14, 1), (11, 1), (9, 2), (10, 2), (12, 2), (13, 2), (14, 2), (15, 1), (9, 3), (8, 3), (11, 2), (10, 3), (15, 2), (9, 4), (12, 3), (13, 3), (14, 3), (11, 3), (15, 3))
+SERVE = (2, 4, 4, 8, 9, 13, 13, 15, 17, 18, 20, 21, 23, 26, 29, 34, 35, 39, 41, 44, 47, 47, 49, 52, 53, 56, 59, 59, 61, 62, 65, 65, 65)
 
 
 class Plan:
@@ -66,17 +66,17 @@
         if hidden == 1536 and heads == 384:
             widths = CHUNKS
         else:
-            widths = (("down", 0, hidden), ("up", 0, hidden), *((n, 0, heads) for n in ("out", "q", "k", "v")), ("vec", 0, 128))
+            widths = (("down", 0, hidden), ("up", 0, hidden), *((n, 0, heads) for n in ("out", "q", "k", "v")))
         chunks = [(name, self.first[name] + off, cw) for name, off, cw in widths]
         chunks = [c + (HOPS[i % len(HOPS)],) for i, c in enumerate(chunks)]
         for _, _, cw, kind in chunks:
             self.z_at.append(self.z_columns)
             self.z_columns += cw if kind[0] == "z" else 0
         self.chunks = chunks
-        self.columns = at + 128
-        self.finish_parts = (8, 4, 1, 1, 1, 1)
+        self.columns = at if self.fused else at + 128
+        self.finish_parts = (2, 1, 1, 1, 1, 1)
         if self.fused:
-            shapes = ((self.share, hidden), (self.share, hidden), (self.share, heads), (3, self.share, heads), (8, self.share))
+            shapes = ((self.share, hidden), (self.share, hidden), (self.share, heads), (3, self.share, heads), (8, 128))
             self.grad_shapes = tuple((a, F32) for a in shapes)
         else:
             self.grad_shapes = (((width, self.columns), BF),)
@@ -92,8 +92,8 @@
         x, wqkv, wout, wup, wdown, gl,
     nrm, q, k, v, prob, ho, resid, gres, glt, n2t, act, glf, vec, work, low_s,
     xs, xr_a, xr_b,
-    g, r1, r2, r3, r4, red, vecs,
-    in_sem, out_sem, red_sem, xsend, xrecv, send, recv,
+    g, r1, r2, r3, r4, red, vmine, vtheirs,
+    in_sem, out_sem, red_sem, xsend, xrecv, send, recv, vsend, vrecv,
     ) = rest
     T, S, D, H, FF = plan.tables, plan.seq, plan.width, plan.heads, plan.hidden
     R = plan.rows
@@ -108,7 +108,8 @@
 
     x_peer, y_peer = chip(zz, yy, 1 - xx), chip(zz, 1 - yy, xx)
     z_peers = [chip(lax.rem(zz + d, 4), yy, xx) for d in (1, 2, 3)]
-    peers = [partner] + ([x_peer, y_peer] + z_peers if plan.fused else [])
+    others = [(lax.rem(dp + d, plan.dp), mp) for d in range(1, plan.dp)] if plan.fused else []
+    peers = [partner] + others
 
     loads = [
         pltpu.make_async_copy(a, b, in_sem.at[i])
@@ -116,7 +117,7 @@
             ((x_hbm, x), (wqkv_hbm, wqkv), (wout_hbm, wout), (cot_hbm, gl), (wup_hbm, wup), (wdown_hbm, wdown))
         )
     ]
-    for c in loads:
+    for c in loads[:2]:
         c.start()
     barrier = pltpu.get_barrier_semaphore()
     for n in peers:
@@ -135,18 +136,13 @@
     def store(i):
         name, c0, cw, _ = plan.chunks[i]
         off = c0 - plan.first[name]
-        if name == "vec":
-            return pltpu.make_async_copy(vecs.at[0:8], grads_hbm[4], red_sem.at[i])
         at = {"down": 0, "up": 1, "out": 2, "q": 3, "k": 3, "v": 3}[name]
         dst = grads_hbm[at].at["qkv".index(name)] if at == 3 else grads_hbm[at]
         return pltpu.make_async_copy(red.at[:, pl.ds(c0, cw)], dst.at[:, pl.ds(off, cw)], red_sem.at[i])
 
     def finished(i, total):
-        name, c0, cw, _ = plan.chunks[i]
-        if name == "vec":
-            vecs[...] = total.T
-        else:
-            red[:, pl.ds(c0, cw)] = total
+        _, c0, cw, _ = plan.chunks[i]
+        red[:, pl.ds(c0, cw)] = total
         store(i).start()
 
     def add(dst, a, b):
@@ -332,6 +328,8 @@
         return pl.ds(pl.multiple_of(b * RB, RB), RB)
 
     loads[0].wait()
+    for c in loads[2:]:
+        c.start()
     g1, b1, g2, b2 = (a[...].reshape(1, D) for a in (g1_ref, b1_ref, g2_ref, b2_ref))
 
     def first_norm(b):
@@ -379,7 +377,7 @@
         for i in range(2):
             part = slice(i * CTX, (i + 1) * CTX)
             s = prob[slot, part, :]
-            e = jnp.exp((s - jnp.max(s, axis=0, keepdims=True)) * scale)
+            e = jnp.exp2((s - jnp.max(s, axis=0, keepdims=True)) * (scale * math.log2(math.e)))
             p = e * (1.0 / jnp.sum(e, axis=0, keepdims=True))
             prob[slot, part, :] = p
             low_s[part, :] = p.astype(BF)
@@ -573,17 +571,17 @@
         rows = slice(t * S, (t + 1) * S)
         ctx = slice(t * S, t * S + CTX)
 
-        def body(j, t=t, rows=rows, ctx=ctx):
+        def body(j, t=t, rows=rows, ctx=ctx, point=point):
             cs = pl.ds(pl.multiple_of(j * 256, 256), 256)
             part = nt(glf[rows, gq : gq + H], wqkv[0, cs, :])
             extra = nt(glf[ctx, gk : gk + H], wqkv[1, cs, :]) + nt(glf[ctx, gv : gv + H], wqkv[2, cs, :])
             xs[ctx, cs] = (part[:CTX] + extra).astype(BF)
             xs[t * S + CTX : (t + 1) * S, cs] = part[CTX:].astype(BF)
+            due_in(j, tiles, point)
 
         loop(tiles, body)
         swap(3, t, xs, xr_a).start()
-        due(point)
-        point += 1
+        point += tiles
 
     def feed_out(t, point):
         rows = slice(t * S, (t + 1) * S)
@@ -591,12 +589,12 @@
         def body(j):
             cs = pl.ds(pl.multiple_of(j * 256, 256), 256)
             nrm[rows, cs] = nn(act[rows, :], wdown[:, cs]).astype(BF)
+            due_in(j, tiles, point)
 
         loop(tiles, body)
-        due(point)
 
     feed_out(0, point)
-    point += 1
+    point += tiles
 
     def first_back(b):
         rs = pl.ds(pl.multiple_of(b * NB, NB), NB)
@@ -615,13 +613,23 @@
     swap(2, 0, nrm, xr_b).start()
     store_gin = pltpu.make_async_copy(gres, gin_hbm, out_sem.at[1])
     store_gin.start()
-    put(plan.first["vec"], 128, jnp.concatenate([vec[...], jnp.zeros((128 - vec.shape[0], D), F32)], axis=0).T)
+    def norm_sums(d):
+        return remote(vmine.at[d], vtheirs.at[d], vsend.at[d], vrecv.at[d], others[d - 1])
+
+    if plan.fused:
+        sums = vec[...]
+        for o in range(plan.dp):
+            vmine[lax.rem(o - dp + plan.dp, plan.dp)] = pltpu.roll(sums, (D - o * plan.share) % D, 1)[:, 0:128]
+        for d in range(1, plan.dp):
+            norm_sums(d).start()
+    else:
+        put(plan.first["vec"], 128, jnp.concatenate([vec[...], jnp.zeros((128 - vec.shape[0], D), F32)], axis=0).T)
     due(point)
     point += 1
 
     for t in range(1, T):
         feed_out(t, point)
-        point += 1
+        point += tiles
         swap(2, t, nrm, xr_b).start()
 
     def output(b):
@@ -640,6 +648,17 @@
     store_out.start()
     assert point == len(SERVE)
     due(point, True)
+    if plan.fused:
+        total = vmine[0]
+        for d in range(1, plan.dp):
+            norm_sums(d).wait_recv()
+            total = total + vtheirs[d]
+        vmine[0] = total
+        store_sums = pltpu.make_async_copy(vmine.at[0], grads_hbm[4], out_sem.at[2])
+        store_sums.start()
+        for d in range(1, plan.dp):
+            norm_sums(d).wait_send()
+        store_sums.wait()
 
     if not plan.fused:
         store = lambda i: pltpu.make_async_copy(g, grads_hbm[0], red_sem.at[0])
@@ -664,10 +683,10 @@
     if plan.fused:
         gshape = (2, 2, 2, 2, share, W)
         comm = [V((2, 2, 2, share, W), BF), V((2, 2, share, W), BF), V((3, share, W), BF)]
-        comm += [V((2, 2, share, plan.z_columns), BF), V((share, W), F32), V((128, share), F32)]
+        comm += [V((2, 2, share, plan.z_columns), BF), V((share, W), F32), V((plan.dp, 8, 128), F32), V((plan.dp, 8, 128), F32)]
     else:
         gshape = (D, W)
-        comm = [V((8, 128), F32)] * 6
+        comm = [V((8, 128), F32)] * 7
     scratch = [
         V((R, D), BF), V((3, D, H), BF), V((H, D), BF), V((D, FF), BF), V((FF, D), BF), V((R, D), BF),
         V((R, D), BF), V((R, H), BF), V((plan.tables * CTX, H), BF), V((plan.tables * CTX, H), BF),
@@ -675,8 +694,8 @@
         V((D, R), BF), V((D, R), BF), V((R, FF), BF), V((R, FF), BF), V((8, D), F32), V((3, R, 256), F32), V((2 * CTX, plan.seq), BF),
         V((R, D), BF), V((R, D), BF), V((R, D), BF),
         V(gshape, BF), *comm,
-        DMA((7,)), DMA((2,)), DMA((n,)), DMA((4, plan.tables)), DMA((4, plan.tables)),
-        DMA((n, 5)), DMA((n, 5)),
+        DMA((7,)), DMA((3,)), DMA((n,)), DMA((4, plan.tables)), DMA((4, plan.tables)),
+        DMA((n, 5)), DMA((n, 5)), DMA((plan.dp,)), DMA((plan.dp,)),
     ]
     hbm = pl.BlockSpec(memory_space=pl.ANY)
 
@@ -701,7 +720,9 @@
 def finish_kernel(plan, *refs):
     n = 6
     src, vec_ref, dst, vec_out = refs[:n], refs[n], refs[n + 1 : 2 * n + 1], refs[2 * n + 1 : 2 * n + 5]
-    bufs, in_sem, out_sem = refs[2 * n + 5 : 3 * n + 5], refs[3 * n + 5], refs[3 * n + 6]
+    bufs, vec_buf, in_sem, out_sem, vec_sem = refs[2 * n + 5 : 3 * n + 5], *refs[3 * n + 5 :]
+    load_vec = pltpu.make_async_copy(vec_ref, vec_buf, vec_sem)
+    load_vec.start()
     moves = []
     for i in range(n):
         rows = src[i].shape[0]
@@ -714,8 +735,9 @@
         stores.append(pltpu.make_async_copy(bufs[i].at[rows], dst[i].at[rows], out_sem.at[m]))
     for c in loads:
         c.start()
+    load_vec.wait()
     for i in range(4):
-        vec_out[i][...] = vec_ref[i, :]
+        vec_out[i][...] = vec_buf[i, 0 : plan.share]
     for a, b in zip(loads, stores):
         a.wait()
         b.start()
@@ -737,10 +759,10 @@
         kernel,
         out_shape=tuple(jax.ShapeDtypeStruct(a.shape, a.dtype) for a in arrays)
         + tuple(jax.ShapeDtypeStruct((share,), F32) for _ in range(4)),
-        in_specs=[hbm] * 6 + [vmem],
+        in_specs=[hbm] * 7,
         out_specs=(hbm,) * 6 + (vmem,) * 4,
         scratch_shapes=[pltpu.VMEM(a.shape, a.dtype) for a in arrays]
-        + [pltpu.SemaphoreType.DMA((n,)), pltpu.SemaphoreType.DMA((n,))],
+        + [pltpu.VMEM(vec.shape, F32), pltpu.SemaphoreType.DMA((n,)), pltpu.SemaphoreType.DMA((n,)), pltpu.SemaphoreType.DMA],
         name="finish",
     )(*arrays, vec)
     return (out.reshape(shape), gin.reshape(shape), jnp.transpose(qkv, (1, 0, 2)), o.T, up, down.T, *norms)

time: 93.8 us -> 90 us (0.959)
  Pallas kernels: 92.7 us -> 89 us
    pallas_call x1, Pallas kernels: 86.4 us -> 83.5 us  [run_layer(): pl.pallas_call(kernel, out_shape=(jax.ShapeDtypeStruct((R, D), BF), jax.S...]
where the time goes in v4:
time: 90 us; the launch traced here: 89.8 us
  Pallas kernels  89 us (99%)
    pallas_call x1, Pallas kernels, run_layer(): pl.pallas_call(kernel, out_shape=(jax.ShapeDtypeStruct((R, D), BF), jax.S...  83.5 us
    pallas_call x1, Pallas kernels, finish(): pl.pallas_call(kernel, out_shape=tuple((jax.ShapeDtypeStruct(a.shape, a.d...  5.44 us

profile of v4, /device:TPU:0, one launch (start us, length us, event | category | flops | bytes accessed | tf_op | source)
XLA Modules:
  0.0 89.8 jit_solution(16800624564012754493)
XLA Ops:
  0.6 83.5 %layer.1 = (bf16[1024,768]{1,0:T(8,128)(2,1)}, f32[1024,768]{1,0:T(8,128)}, f32[48,1536]{1,0:T(8,128)}, f32[48,1536]{1,0:T(8,128)}, f32[48,384]{1,0:T(8,128)}, /*index=5*/f32[3,48,384]{2,1,0:T(8,128)}, f32[8,128]{1,0:T(8,128)}) custom-call(s32[2]{0:T(128)} %refs_0_.1, bf16[1024,768]{1,0:T(8,128)(2,1)} %bitcast.9, bf16[3,768,384]{2,1,0:T(8,128)(2,1)} %bitcast.8, ...), custom_call_target="tpu_custom_call" | custom-call | tf_op jit(solution)/shard_map/layer/pallas_call | solution.py:705
  84.2 5.4 %finish.1 = (f32[1024,768]{1,0:T(8,128)}, bf16[1024,768]{1,0:T(8,128)(2,1)}, f32[48,1536]{1,0:T(8,128)}, f32[48,1536]{1,0:T(8,128)}, f32[3,48,384]{2,1,0:T(8,128...) custom-call(f32[1024,768]{1,0:T(8,128)} %get-tuple-element.27.refs_0_, ...), custom_call_target="tpu_custom_call" | custom-call | tf_op jit(solution)/shard_map/finish/pallas_call | solution.py:758

commit v5 on v4

--- a/solution.py
+++ b/solution.py
@@ -418,7 +418,10 @@
 
     for t in range(T):
         swap(0, t, xs, xr_a).wait_recv()
-        loop(per, lambda i, t=t: second_norm(t * per + i))
+        for i in range(per):
+            second_norm(t * per + i)
+        for b in range(t * per, (t + 1) * per):
+            n2t[:, b * RB : (b + 1) * RB] = n2[b * RB : (b + 1) * RB, :].T
     loads[4].wait()
     loads[5].wait()
 
@@ -462,8 +465,6 @@
         grad(plan.first["up"] + off, n2t, glf, hidden_of(c), step)
         due_in(c, steps, 0)
 
-    for b in range(R // RB):
-        n2t[:, b * RB : (b + 1) * RB] = n2[b * RB : (b + 1) * RB, :].T
     loop(steps, feed)
     point = steps
 
@@ -720,7 +721,8 @@
 def finish_kernel(plan, *refs):
     n = 6
     src, vec_ref, dst, vec_out = refs[:n], refs[n], refs[n + 1 : 2 * n + 1], refs[2 * n + 1 : 2 * n + 5]
-    bufs, vec_buf, in_sem, out_sem, vec_sem = refs[2 * n + 5 : 3 * n + 5], *refs[3 * n + 5 :]
+    bufs, vec_buf, in_sem, out_sem, vec_sem, row_sem = refs[2 * n + 5 : 3 * n + 5], *refs[3 * n + 5 : 3 * n + 10]
+    rows_buf = refs[3 * n + 10 :]
     load_vec = pltpu.make_async_copy(vec_ref, vec_buf, vec_sem)
     load_vec.start()
     moves = []
@@ -737,7 +739,9 @@
         c.start()
     load_vec.wait()
     for i in range(4):
-        vec_out[i][...] = vec_buf[i, 0 : plan.share]
+        rows_buf[i][...] = vec_buf[i, 0 : plan.share]
+        stores.append(pltpu.make_async_copy(rows_buf[i], vec_out[i], row_sem.at[i]))
+        stores[-1].start()
     for a, b in zip(loads, stores):
         a.wait()
         b.start()
@@ -760,9 +764,10 @@
         out_shape=tuple(jax.ShapeDtypeStruct(a.shape, a.dtype) for a in arrays)
         + tuple(jax.ShapeDtypeStruct((share,), F32) for _ in range(4)),
         in_specs=[hbm] * 7,
-        out_specs=(hbm,) * 6 + (vmem,) * 4,
+        out_specs=(hbm,) * 10,
         scratch_shapes=[pltpu.VMEM(a.shape, a.dtype) for a in arrays]
-        + [pltpu.VMEM(vec.shape, F32), pltpu.SemaphoreType.DMA((n,)), pltpu.SemaphoreType.DMA((n,)), pltpu.SemaphoreType.DMA],
+        + [pltpu.VMEM(vec.shape, F32), pltpu.SemaphoreType.DMA((n,)), pltpu.SemaphoreType.DMA((n,)), pltpu.SemaphoreType.DMA, pltpu.SemaphoreType.DMA((4,))]
+        + [pltpu.VMEM((share,), F32)] * 4,
         name="finish",
     )(*arrays, vec)
     return (out.reshape(shape), gin.reshape(shape), jnp.transpose(qkv, (1, 0, 2)), o.T, up, down.T, *norms)

time: 90 us -> 89.2 us (level)
  no operation moved by 1% of the time
where the time goes in v5:
time: 89.2 us; the launch traced here: 89 us
  Pallas kernels  88.2 us (99%)
    pallas_call x1, Pallas kernels, run_layer(): pl.pallas_call(kernel, out_shape=(jax.ShapeDtypeStruct((R, D), BF), jax.S...  83.2 us
    pallas_call x1, Pallas kernels, finish(): pl.pallas_call(kernel, out_shape=tuple((jax.ShapeDtypeStruct(a.shape, a.d...  4.97 us

profile of v5, /device:TPU:0, one launch (start us, length us, event | category | flops | bytes accessed | tf_op | source)
XLA Modules:
  0.0 89.0 jit_solution(5430539604677215720)
XLA Ops:
  0.6 83.2 %layer.1 = (bf16[1024,768]{1,0:T(8,128)(2,1)}, f32[1024,768]{1,0:T(8,128)}, f32[48,1536]{1,0:T(8,128)}, f32[48,1536]{1,0:T(8,128)}, f32[48,384]{1,0:T(8,128)}, /*index=5*/f32[3,48,384]{2,1,0:T(8,128)}, f32[8,128]{1,0:T(8,128)}) custom-call(s32[2]{0:T(128)} %refs_0_.1, bf16[1024,768]{1,0:T(8,128)(2,1)} %bitcast.9, bf16[3,768,384]{2,1,0:T(8,128)(2,1)} %bitcast.8, ...), custom_call_target="tpu_custom_call" | custom-call | tf_op jit(solution)/shard_map/layer/pallas_call | solution.py:706
  83.9 5.0 %finish.1 = (f32[1024,768]{1,0:T(8,128)}, bf16[1024,768]{1,0:T(8,128)(2,1)}, f32[48,1536]{1,0:T(8,128)}, f32[48,1536]{1,0:T(8,128)}, f32[3,48,384]{2,1,0:T(8,128...) custom-call(f32[1024,768]{1,0:T(8,128)} %get-tuple-element.27.refs_0_, ...), custom_call_target="tpu_custom_call" | custom-call | tf_op jit(solution)/shard_map/finish/pallas_call | solution.py:762
